TPU v7x, 128 devices: a whole 4x4x4 slice. The times are simulated.
128 devices in a mesh: energy: 32 (over z, y, core), space: 4 (over x).
Axes of the slice: x: 4, y: 4, z: 4, core: 2. Of those that a mesh axis runs over, the one named last changes fastest.
Arguments:
- ham_diag: float32 [4, 256, 256], P('space')
- ham_coup: float32 [4, 256, 256], P('space'), may hold values from -0.1875 to 0.1875
- energies: float32 [32], P('energy'), may hold values from 1 to 2
- pattern: int32 [4, 43264], P('space'), may hold values from 0 to 65535, as said below
- coulomb: float32 [4, 43264], P('space', 'energy'), may hold values from 0.5 to 2
Outputs:
- green: float32 [32, 4, 256, 256], P('energy', 'space')
- screened: float32 [32, 4, 43264], P(None, 'space', 'energy')
Inputs may be any that keep to these rules, and one draw needn't show every extreme that they name: `pattern`: each row holds 43264 distinct flat positions of one block, among them all 256 diagonal positions.
All inputs are finite; a program needn't handle non-finite values.
Results may differ from a plain program's by a relative error of at most 0.0001.
Values sent between devices are 32-bit elements; how exact they have to be, the bound alone decides.
A program may use at most 128 MiB of HBM per device.

v0:
```python
import jax
import jax.numpy as jnp
from jax import lax
from jax.sharding import PartitionSpec as P

polar_coef = 128.0
sigma_coef = 0.5


def shifted(value, axis, steps):
    count = lax.axis_size(axis)
    initial, last = (max(0, -steps), min(count, count - steps))
    return lax.ppermute(value, axis, [(source, source + steps) for source in range(initial, last)])


def tri_solve(factor, target, flipped):
    return lax.linalg.triangular_solve(
        factor, target, left_side=True, lower=True, transpose_a=flipped
    )


def invert_spd(matrix):
    ident = jnp.broadcast_to(jnp.eye(matrix.shape[-1], dtype=matrix.dtype), matrix.shape)
    factor = jnp.linalg.cholesky(matrix)
    return tri_solve(factor, tri_solve(factor, ident, False), True)


def left_segment(incoming, systems, couplings):

    def advance(incoming_term, block_pair):
        system, coupling = block_pair
        factor = jnp.linalg.cholesky(system - incoming_term)
        solved = tri_solve(factor, coupling, False)
        return (jnp.dot(solved.T, solved, precision=lax.Precision.HIGHEST), incoming_term)

    outgoing, left_terms = lax.scan(advance, incoming, (systems, couplings))
    return (left_terms, outgoing)


def right_segment(incoming_factor, systems, couplings):

    def retreat(factor, block_pair):
        system, coupling = block_pair
        solved = tri_solve(factor, coupling.T, False)
        rights = jnp.dot(solved.T, solved, precision=lax.Precision.HIGHEST)
        return (jnp.linalg.cholesky(system - rights), rights)

    outgoing, right_terms = lax.scan(retreat, incoming_factor, (systems, couplings), reverse=True)
    return (right_terms, outgoing)


def screen_entries(samples, coulomb, width):
    count = samples.shape[0]
    length = 2 * count
    flat = samples.reshape(count, -1)
    freq_index = jnp.arange(length, dtype=jnp.int32)[:, None]
    time_index = jnp.arange(count, dtype=jnp.int32)[None, :]
    phase = 2.0 * jnp.pi / length * (freq_index * time_index % length).astype(jnp.float32)
    fwd_cos = jnp.cos(phase)
    fwd_sin = jnp.sin(phase)
    inv_cos = fwd_cos.T / length
    inv_sin = fwd_sin.T / length
    highest = lax.Precision.HIGHEST
    green_cos = jnp.dot(fwd_cos, flat, precision=highest)
    green_sin = jnp.dot(fwd_sin, flat, precision=highest)
    power = green_cos * green_cos + green_sin * green_sin
    polar = jnp.dot(inv_cos, power, precision=highest) * (polar_coef * width / count)
    scaled = coulomb * polar
    screened = coulomb / jnp.sqrt(1.0 + scaled * scaled)
    screen_cos = jnp.dot(fwd_cos, screened, precision=highest)
    screen_sin = jnp.dot(fwd_sin, screened, precision=highest)
    real_part = green_cos * screen_cos - green_sin * screen_sin
    imag_part = green_cos * screen_sin + green_sin * screen_cos
    selfen = jnp.dot(inv_cos, real_part, precision=highest) + jnp.dot(
        inv_sin, imag_part, precision=highest
    )
    selfen = selfen * (sigma_coef / count)
    return (screened.reshape(samples.shape), selfen.reshape(samples.shape))


def on_device(ham_diag, ham_coup, energies, pattern, coulomb):
    blocks = ham_diag.shape[0]
    width = ham_diag.shape[1]
    per_energy = energies.shape[0]
    spaces = lax.axis_size("space")
    place = lax.axis_index("space")
    ident = jnp.eye(width, dtype=jnp.float32)
    two_ident = 2.0 * ident
    systems = ham_diag[None] + energies[:, None, None, None] * ident
    left_store = jnp.zeros((per_energy, blocks, width, width), jnp.float32)
    right_store = jnp.zeros((per_energy, blocks, width, width), jnp.float32)
    left_in = jnp.zeros((width, width), jnp.float32)
    right_in = jnp.zeros((width, width), jnp.float32)
    sections = per_energy + spaces - 1
    for section_index in range(sections):
        left_pick = section_index - place
        right_pick = section_index - (spaces - 1 - place)
        left_valid = jnp.logical_and(left_pick >= 0, left_pick < per_energy)
        right_valid = jnp.logical_and(right_pick >= 0, right_pick < per_energy)
        left_at = jnp.clip(left_pick, 0, per_energy - 1)
        right_at = jnp.clip(right_pick, 0, per_energy - 1)
        left_system = lax.dynamic_index_in_dim(systems, left_at, 0, keepdims=False)
        left_terms, left_out = left_segment(left_in, left_system, ham_coup)
        left_store = jnp.where(
            left_valid,
            lax.dynamic_update_index_in_dim(left_store, left_terms, left_at, 0),
            left_store,
        )
        use_lead = jnp.logical_or(place == spaces - 1, jnp.logical_not(right_valid))
        start_factor = jnp.where(use_lead, two_ident, right_in)
        right_system = lax.dynamic_index_in_dim(systems, right_at, 0, keepdims=False)
        right_terms, right_out = right_segment(start_factor, right_system, ham_coup)
        right_store = jnp.where(
            right_valid,
            lax.dynamic_update_index_in_dim(right_store, right_terms, right_at, 0),
            right_store,
        )
        if section_index + 1 < sections:
            left_in = shifted(left_out, "space", 1)
            right_in = shifted(right_out, "space", -1)
    reduced = systems - left_store - right_store
    base = invert_spd(reduced)
    flat = base.reshape(per_energy, blocks, width * width)
    samples = jnp.take_along_axis(flat, pattern[None], axis=2)
    gathered = lax.all_to_all(samples, "energy", split_axis=2, concat_axis=0, tiled=True)
    screened, selfen = screen_entries(gathered, coulomb, width)
    returned = lax.all_to_all(selfen, "energy", split_axis=0, concat_axis=2, tiled=True)

    def place_row(row_values, positions):
        return jnp.zeros((width * width,), jnp.float32).at[positions].set(row_values)

    spread = jax.vmap(jax.vmap(place_row, (0, 0)), (0, None))(returned, pattern)
    spread = spread.reshape(per_energy, blocks, width, width)
    sym = 0.5 * (spread + jnp.swapaxes(spread, 2, 3))
    green = invert_spd(reduced - sym)
    return (green, screened)


def solution(mesh):
    return jax.shard_map(
        on_device,
        mesh=mesh,
        in_specs=(
            P("space", None, None),
            P("space", None, None),
            P("energy"),
            P("space", None),
            P("space", "energy"),
        ),
        out_specs=(P("energy", "space", None, None), P(None, "space", "energy")),
        check_vma=False,
    )
```

profile of v0, /device:TPU:1, one launch (start us, length us, event | category | flops | bytes accessed | tf_op | source)
XLA Modules:
  0.0 1695.7 jit_solution(14433259118090636683)
XLA Ops:
  5.1 19.9 %custom-call.49 = f32[2,128,128]{1,2,0:T(8,128)S(1)} custom-call(f32[2,128,128]{2,1,0:T(8,128)S(1)} %get-tuple-element.202), custom_call_target="InvertDiagBlocksLowerTriangular" | custom-call | tf_op jit(solution)/shard_map/while/body/eval_jaxpr/triangular_solve/custom-call.5 | solution.py:17
  30.6 11.7 cholesky.525
  52.6 11.7 cholesky.542
  91.1 11.7 cholesky.440
  109.7 19.7 %custom-call.44 = f32[2,128,128]{1,2,0:T(8,128)S(1)} custom-call(f32[2,128,128]{2,1,0:T(8,128)S(1)} %get-tuple-element.199), custom_call_target="InvertDiagBlocksLowerTriangular" | custom-call | tf_op jit(solution)/shard_map/while/body/eval_jaxpr/triangular_solve/custom-call.5 | solution.py:17
  145.4 19.9 %custom-call.51 = f32[2,128,128]{1,2,0:T(8,128)S(1)} custom-call(f32[2,128,128]{2,1,0:T(8,128)S(1)} %get-tuple-element.203), custom_call_target="InvertDiagBlocksLowerTriangular" | custom-call | tf_op jit(solution)/shard_map/while/body/eval_jaxpr/triangular_solve/custom-call.5 | solution.py:17
  190.9 11.7 cholesky.576
  229.6 11.7 cholesky.474
  247.9 19.7 %custom-call.46 = f32[2,128,128]{1,2,0:T(8,128)S(1)} custom-call(f32[2,128,128]{2,1,0:T(8,128)S(1)} %get-tuple-element.200), custom_call_target="InvertDiagBlocksLowerTriangular" | custom-call | tf_op jit(solution)/shard_map/while/body/eval_jaxpr/triangular_solve/custom-call.5 | solution.py:17
  278.0 19.9 %custom-call.53 = f32[2,128,128]{1,2,0:T(8,128)S(1)} custom-call(f32[2,128,128]{2,1,0:T(8,128)S(1)} %get-tuple-element.204), custom_call_target="InvertDiagBlocksLowerTriangular" | custom-call | tf_op jit(solution)/shard_map/while/body/eval_jaxpr/triangular_solve/custom-call.5 | solution.py:17
  321.7 11.7 cholesky.610
  360.4 11.7 cholesky.508
  378.8 19.7 %custom-call.48 = f32[2,128,128]{1,2,0:T(8,128)S(1)} custom-call(f32[2,128,128]{2,1,0:T(8,128)S(1)} %get-tuple-element.201), custom_call_target="InvertDiagBlocksLowerTriangular" | custom-call | tf_op jit(solution)/shard_map/while/body/eval_jaxpr/triangular_solve/custom-call.5 | solution.py:17
  410.1 19.8 %custom-call.55 = f32[2,128,128]{1,2,0:T(8,128)S(1)} custom-call(f32[2,128,128]{2,1,0:T(8,128)S(1)} %get-tuple-element.205), custom_call_target="InvertDiagBlocksLowerTriangular" | custom-call | tf_op jit(solution)/shard_map/while/body/eval_jaxpr/triangular_solve/custom-call.5 | solution.py:17
  453.9 11.7 custom-call.58
  472.5 19.9 %custom-call.60 = f32[1,1,2,128,128]{3,4,2,1,0:T(8,128)S(1)} custom-call(f32[1,1,2,128,128]{4,3,2,1,0:T(8,128)S(1)} %bitcast.426), custom_call_target="InvertDiagBlocksLowerTriangular" | custom-call | tf_op jit(solution)/shard_map/triangular_solve/custom-call.8 | solution.py:17
  494.3 221.6 %gather_fusion = f32[43264]{0:T(1024)S(1)} fusion(f32[65536]{0:T(1024)S(1)} %bitcast.405, s32[44032]{0:T(1024)S(1)} %pad_clamp_fusion), kind=kCustom, calls=%fused_computation | custom fusion | bytes 519168 | tf_op jit(solution)/shard_map/jit(take_along_axis)/gather | solution.py:124
  716.3 31.1 %copy.149 = f32[1,1,43264]{1,0,2:T(1,128)} copy(f32[1,1,43264]{2,1,0:T(1,128)S(1)} %and_select_fusion) | data formatting | bytes 346112 | tf_op jit(solution)/shard_map/jit(take_along_axis)/select_n | solution.py:124
  747.9 324.0 %reduce.34 = f32[43264]{0:T(1024)S(1)} reduce(f32[43264,1,1]{2,1,0:T(1,128)} %bitcast.406, f32[]{:T(128)} %broadcast.495), dimensions={1,2}, to_apply=%bitcast.288.reduce_sub_computation | reduce | bytes 346116
  1093.1 39.4 %reshape.599 = f32[43264,1,1]{2,1,0:T(1,128)} reshape(f32[32,1352]{1,0:T(8,128)S(1)} %reduce.35) | data formatting | bytes 346112
  1132.5 323.5 %bitcast_reduce_fusion = f32[43264]{0:T(1024)S(1)} fusion(f32[43264,1,1]{2,1,0:T(1,128)} %reshape.599), kind=kLoop, calls=%fused_computation.382 | loop fusion | bytes 346112 | tf_op jit(solution)/shard_map/all_to_all | solution.py:125
  1473.3 158.6 %scatter_custom_fusion = f32[65536]{0:T(1024)S(1)} fusion(s32[43264]{0:T(1024)S(1)} %broadcast_select_fusion, f32[43264]{0:T(1024)S(1)} %reshape.527, f32[]{:T(128)} %constant.286.clone.1), kind=kCustom, calls=%fused_computation.151 | custom fusion | bytes 262148
  1654.4 11.7 custom-call.63
  1673.3 19.7 %custom-call.65 = f32[1,1,2,128,128]{3,4,2,1,0:T(8,128)S(1)} custom-call(f32[1,1,2,128,128]{4,3,2,1,0:T(8,128)S(1)} %bitcast.425), custom_call_target="InvertDiagBlocksLowerTriangular" | custom-call | tf_op jit(solution)/shard_map/triangular_solve/custom-call.8 | solution.py:17
  (307 shorter events, 337.7 us)
Async XLA Ops:
  0.6 266.9 %copy-start = (f32[1,256,256]{2,1,0:T(8,128)S(1)}, f32[1,256,256]{2,1,0:T(8,128)}, u32[]{:S(2)}) copy-start(f32[1,256,256]{2,1,0:T(8,128)} %param.14) | copy-start | bytes 786436
  67.3 73.4 %collective-permute-start.3 = (f32[256,256]{0,1:T(8,128)S(1)}, f32[256,256]{0,1:T(8,128)S(1)}, u32[]{:S(2)}, u32[]{:S(2)}) collective-permute-start(f32[256,256]{0,1:T(8,128)S(1)} %fusion.68), channel_id=1, source_target_pairs={{1,0},{2,1},{3,2},{5,4},{6,5},{7,6},{9,8},{10,9},{11,10},{13,12},{... | collective-permute-start | bytes 786440 | tf_op jit(solution)/shard_map/ppermute | solution.py:13
  132.7 35.4 %collective-permute-start = (f32[256,256]{0,1:T(8,128)S(1)}, f32[256,256]{0,1:T(8,128)S(1)}, u32[]{:S(2)}, u32[]{:S(2)}) collective-permute-start(f32[256,256]{0,1:T(8,128)S(1)} %fusion.31), channel_id=1, source_target_pairs={{0,1},{1,2},{2,3},{4,5},{5,6},{6,7},{8,9},{9,10},{10,11},{12,13},{... | collective-permute-start | bytes 786440 | tf_op jit(solution)/shard_map/ppermute | solution.py:13
  205.6 68.1 %collective-permute-start.4 = (f32[256,256]{0,1:T(8,128)S(1)}, f32[256,256]{0,1:T(8,128)S(1)}, u32[]{:S(2)}, u32[]{:S(2)}) collective-permute-start(f32[256,256]{0,1:T(8,128)S(1)} %fusion.69), channel_id=1, source_target_pairs={{1,0},{2,1},{3,2},{5,4},{6,5},{7,6},{9,8},{10,9},{11,10},{13,12},{... | collective-permute-start | bytes 786440 | tf_op jit(solution)/shard_map/ppermute | solution.py:13
  269.8 29.1 %collective-permute-start.1 = (f32[256,256]{0,1:T(8,128)}, f32[256,256]{0,1:T(8,128)S(1)}, u32[]{:S(2)}, u32[]{:S(2)}) collective-permute-start(f32[256,256]{0,1:T(8,128)} %fusion.35), channel_id=1, source_target_pairs={{0,1},{1,2},{2,3},{4,5},{5,6},{6,7},{8,9},{9,10},{10,11},{12,13},{... | collective-permute-start | bytes 786440 | tf_op jit(solution)/shard_map/ppermute | solution.py:13
  336.5 68.2 %collective-permute-start.5 = (f32[256,256]{0,1:T(8,128)S(1)}, f32[256,256]{0,1:T(8,128)}, u32[]{:S(2)}, u32[]{:S(2)}) collective-permute-start(f32[256,256]{0,1:T(8,128)S(1)} %fusion.70), channel_id=1, source_target_pairs={{1,0},{2,1},{3,2},{5,4},{6,5},{7,6},{9,8},{10,9},{11,10},{13,12},{... | collective-permute-start | bytes 786440 | tf_op jit(solution)/shard_map/ppermute | solution.py:13
  400.0 30.9 %collective-permute-start.2 = (f32[256,256]{0,1:T(8,128)S(1)}, f32[256,256]{0,1:T(8,128)}, u32[]{:S(2)}, u32[]{:S(2)}) collective-permute-start(f32[256,256]{0,1:T(8,128)S(1)} %fusion.39), channel_id=1, source_target_pairs={{0,1},{1,2},{2,3},{4,5},{5,6},{6,7},{8,9},{9,10},{10,11},{12,13},{... | collective-permute-start | bytes 786440 | tf_op jit(solution)/shard_map/ppermute | solution.py:13
  494.3 221.6 %copy-start.1 = (s32[1,43264]{1,0:T(1,128)S(1)}, s32[1,43264]{1,0:T(1,128)}, u32[]{:S(2)}) copy-start(s32[1,43264]{1,0:T(1,128)} %param.16) | copy-start | bytes 519172
  716.3 367.8 %copy-start.3 = (s32[2]{0:T(128)S(1)}, s32[2]{0:T(128)}, u32[]{:S(2)}) copy-start(s32[2]{0:T(128)} %constant.312) | copy-start | bytes 28
  716.3 368.4 %copy-start.2 = (s32[2]{0:T(128)S(1)}, s32[2]{0:T(128)}, u32[]{:S(2)}) copy-start(s32[2]{0:T(128)} %constant.315) | copy-start | bytes 28
  1072.9 19.2 %all-to-all-start = ((f32[32,1,1352]{2,1,0:T(1,128)}), f32[32,1,1352]{2,1,0:T(1,128)S(1)}, u32[]{:S(2)}, u32[]{:S(2)}) async-start(f32[32,1,1352]{2,1,0:T(1,128)} %reshape.598), calls=%async_computation | async-start | bytes 360448 | tf_op jit(solution)/shard_map/all_to_all | solution.py:125
  1460.8 11.9 all-to-all-start.1
where the time goes:
time: 1700 us
  local copies, waits for them, and re-layouts  818 us (48%)
  other arithmetic  788 us (46%)
  starting transfers between devices  33.4 us (2%)
  matrix products  27.9 us (2%)
    unnamed x6, other arithmetic  326 us
    all_to_all x1, local copies, waits for them, and re-layouts, on_device(): lax.all_to_all(samples, 'energy', split_axis=2, concat_axis=0, tiled=True)  324 us
    gather x1, local copies, waits for them, and re-layouts, on_device(): samples = jnp.take_along_axis(flat, pattern[None], axis=2)  222 us
    unnamed x15, local copies, waits for them, and re-layouts  202 us
    another operation x20, other arithmetic, tri_solve(): lax.linalg.triangular_solve(factor, target, left_side=True, lower=True, t...  180 us
    another operation x21, other arithmetic, advance(): factor = jnp.linalg.cholesky(system - incoming_term)  104 us
    another operation x21, other arithmetic, retreat(): return (jnp.linalg.cholesky(system - rights), rights)  104 us
    another operation x14, other arithmetic, invert_spd(): factor = jnp.linalg.cholesky(matrix)  69.3 us
  transfers between devices with their start and end apart: 8, of which 2 were waited for; matrix products, arithmetic and copies ran while one was open for 16% of the time, Pallas kernels for 0%

commit v1 on v0

v1 whole, which is shorter than its diff:
```python
import functools

import jax
import jax.numpy as jnp
from jax import lax
from jax.experimental import pallas as pl
from jax.experimental.pallas import tpu as pltpu
from jax.sharding import PartitionSpec as P

F32, BF16 = jnp.float32, jnp.bfloat16
MESH = pl.DeviceIdType.MESH
VMEM = pltpu.VMEM
DMA = pltpu.SemaphoreType.DMA

polar_coef = 128.0
sigma_coef = 0.5

START_DOUBLINGS = 5
MAX_STEPS = 48
TOLERANCE = 1e-6


def split(value):
    high = value.astype(BF16)
    return high, (value - high.astype(F32)).astype(BF16)


def dot(a, b):
    return jnp.dot(a, b, preferred_element_type=F32)


def dot_nt(a, b):
    return lax.dot_general(a, b, (((1,), (1,)), ((), ())), preferred_element_type=F32)


def mul(a, b):
    return dot(a[0], b[0]) + (dot(a[0], b[1]) + dot(a[1], b[0]))


def product(a, b):
    return mul(split(a), split(b))


def identity(width):
    rows = lax.broadcasted_iota(jnp.int32, (width, width), 0)
    cols = lax.broadcasted_iota(jnp.int32, (width, width), 1)
    return jnp.where(rows == cols, 1.0, 0.0).astype(F32)


def cold_start(matrix):
    ident = identity(matrix.shape[0])
    bound = jnp.max(jnp.sum(jnp.abs(matrix), axis=0, keepdims=True), axis=1, keepdims=True)
    alpha = 1.9 / bound
    power = ident - matrix * alpha
    guess = (ident + power) * alpha
    for _ in range(START_DOUBLINGS):
        high = power.astype(BF16)
        power = dot(high, high)
        guess = guess + dot(guess.astype(BF16), power.astype(BF16))
    return guess


def eliminate(matrix, out_ref):
    width = matrix.shape[0]
    out_ref[...] = matrix
    lanes = lax.broadcasted_iota(jnp.int32, (1, width), 1)

    def step(pivot, carry):
        whole = out_ref[...]
        row = out_ref[pl.ds(pivot, 1), :]
        here = lanes == pivot
        value = jnp.sum(jnp.where(here, row, 0.0), axis=1, keepdims=True)
        column = jnp.sum(jnp.where(here, whole, 0.0), axis=1, keepdims=True)
        scaled = jnp.where(here, 1.0, row) / value
        out_ref[...] = jnp.where(here, 0.0, whole) - column * scaled
        out_ref[pl.ds(pivot, 1), :] = scaled
        return carry

    lax.fori_loop(0, width, step, 0)


def settle(matrices, refs):
    ident = identity(matrices[0].shape[0])
    parts = [split(matrix) for matrix in matrices]

    def unsettled(carry):
        steps, worst = carry
        return jnp.logical_and(worst > TOLERANCE, steps < MAX_STEPS)

    def step(carry):
        worst = jnp.float32(0.0)
        for own, ref in zip(parts, refs):
            guess = ref[...]
            guess_parts = split(guess)
            residual = ident - mul(own, guess_parts)
            ref[...] = guess + dot(guess_parts[0], residual.astype(BF16))
            worst = jnp.maximum(worst, jnp.sum(residual * residual))
        return carry[0] + 1, worst

    steps, worst = lax.while_loop(unsettled, step, (jnp.int32(0), jnp.float32(1.0)))

    @pl.when(jnp.logical_not(worst <= TOLERANCE))
    def _():
        for matrix, ref in zip(matrices, refs):
            eliminate(matrix, ref)


def invert(matrices, refs):
    for matrix, ref in zip(matrices, refs):
        ref[...] = cold_start(matrix)
    settle(matrices, refs)


def send_blocks(count, me, source, target, send_sems, recv_sems):
    def one(step, carry):
        peer = lax.rem(me + step, count)
        pltpu.make_async_remote_copy(
            src_ref=source(peer), dst_ref=target(me),
            send_sem=send_sems.at[step], recv_sem=recv_sems.at[me],
            device_id={"energy": peer}, device_id_type=MESH,
        ).start()
        return carry

    lax.fori_loop(1, count, one, 0)


def await_blocks(count, me, source, target, send_sems, recv_sems):
    def one(step, carry):
        peer = lax.rem(me + step, count)
        copy = pltpu.make_async_remote_copy(
            src_ref=source(peer), dst_ref=target(peer),
            send_sem=send_sems.at[step], recv_sem=recv_sems.at[peer],
            device_id={"energy": peer}, device_id_type=MESH,
        )
        copy.wait_send()
        copy.wait_recv()
        return carry

    lax.fori_loop(1, count, one, 0)


def greet_energy(count, me, barrier):
    def one(step, carry):
        pl.semaphore_signal(barrier, inc=1, device_id={"energy": lax.rem(me + step, count)}, device_id_type=MESH)
        return carry

    lax.fori_loop(1, count, one, 0)


def collect_kernel(
    count, spaces, diag_ref, coup_ref, pattern_ref, bare_ref,
    diags_ref, coups_ref, rows_ref, slots_ref, bare_pos_ref, bare_own_ref,
    own_pattern, partial, arrived, own_sem, far_send, far_recv, near_send, near_recv, send_sems, recv_sems,
):
    me = lax.axis_index("energy")
    place = lax.axis_index("space")
    width = diag_ref.shape[1]
    half = width // 2
    core = lax.rem(me, 2)
    other = me + 1 - 2 * core
    chunk = bare_ref.shape[1]
    span = 1352

    barrier = pltpu.get_barrier_semaphore()
    greet_energy(count, me, barrier)
    for step in range(1, spaces):
        pl.semaphore_signal(
            barrier, inc=1, device_id={"space": lax.rem(place + step, spaces)}, device_id_type=MESH)
    pl.semaphore_wait(barrier, count + spaces - 2)

    own_half = pl.ds(pl.multiple_of(core * half, half), half)
    other_half = pl.ds(pl.multiple_of((1 - core) * half, half), half)

    def far_copy(step, kind):
        source, store = ((diag_ref, diags_ref), (coup_ref, coups_ref))[kind]
        return pltpu.make_async_remote_copy(
            src_ref=source.at[0, own_half], dst_ref=store.at[place, own_half],
            send_sem=far_send.at[step, kind], recv_sem=far_recv.at[step, kind],
            device_id={"space": lax.rem(place + step, spaces)}, device_id_type=MESH)

    def near_copy(step, kind):
        store = (diags_ref, coups_ref)[kind]
        source = lax.rem(place + spaces - step, spaces)
        return pltpu.make_async_remote_copy(
            src_ref=store.at[source, own_half], dst_ref=store.at[source, own_half],
            send_sem=near_send.at[step, kind], recv_sem=near_recv.at[step, kind],
            device_id={"energy": other}, device_id_type=MESH)

    order = (1, 3, 2)
    for step in order:
        for kind in range(2):
            far_copy(step, kind).start()
    own_copies = [
        pltpu.make_async_copy(diag_ref.at[0], diags_ref.at[place], own_sem.at[0]),
        pltpu.make_async_copy(coup_ref.at[0], coups_ref.at[place], own_sem.at[1]),
    ]
    for copy in own_copies:
        copy.start()

    for part in range(count):
        piece = pattern_ref[:, part * span:part * span + chunk]
        own_pattern[part] = piece
        row = lax.shift_right_logical(piece, 8)
        col = jnp.bitwise_and(piece, 255)
        high = jnp.maximum(row, col)
        low = jnp.minimum(row, col)
        lower = low >= 128
        pivot = high == low
        rows_ref[part] = jnp.where(jnp.logical_and(lower, jnp.logical_not(pivot)), low - 128, high)
        slots_ref[part] = jnp.where(lower, jnp.where(pivot, 128, high - 128), low)
    mine = own_pattern[me]
    bare = bare_ref[...]
    index = lax.broadcasted_iota(jnp.int32, (width, chunk), 0)
    on_row = index == lax.shift_right_logical(mine, 8)
    on_col = jnp.where(index == jnp.bitwise_and(mine, 255), 1.0, 0.0).astype(BF16)
    rest = bare
    total = None
    for _ in range(3):
        part = rest.astype(BF16).astype(F32)
        rest = rest - part
        term = dot_nt(jnp.where(on_row, part, 0.0).astype(BF16), on_col)
        total = term if total is None else total + term
    partial[...] = total
    for line in range(chunk // 128):
        bare_own_ref[line:line + 1, :] = bare[:, line * 128:(line + 1) * 128]
    for line in range(chunk // 128, bare_own_ref.shape[0]):
        bare_own_ref[line:line + 1, :] = jnp.zeros((1, 128), F32)

    source = lambda peer: partial.at[pl.ds(pl.multiple_of(peer * 8, 8), 8), :]
    target = lambda peer: arrived.at[peer]
    send_blocks(count, me, source, target, send_sems, recv_sems)
    arrived[me] = partial[pl.ds(pl.multiple_of(me * 8, 8), 8), :]

    for step in order:
        for kind in range(2):
            copy = far_copy(step, kind)
            copy.wait_recv()
            near_copy(step, kind).start()
    await_blocks(count, me, source, target, send_sems, recv_sems)
    pieces = [arrived[peer] for peer in range(count)]
    while len(pieces) > 1:
        pieces = [pieces[i] + pieces[i + 1] for i in range(0, len(pieces), 2)]
    bare_pos_ref[...] = pieces[0]
    for copy in own_copies:
        copy.wait()
    for step in order:
        for kind in range(2):
            far_copy(step, kind).wait_send()
            near_copy(step, kind).wait_send()
            store = (diags_ref, coups_ref)[kind]
            block = lax.rem(place + spaces - step, spaces)
            pltpu.make_async_remote_copy(
                src_ref=store.at[block, other_half], dst_ref=store.at[block, other_half],
                send_sem=near_send.at[step, kind], recv_sem=near_recv.at[step, kind],
                device_id={"energy": other}, device_id_type=MESH).wait_recv()


def chain_kernel(
    place_ref, shift_ref, diags_ref, coups_ref, reduced_ref, base_ref,
    u_ref, ut_ref, v_ref, vt_ref, w_ref, wt_ref, c_ref, ct_ref, last_ref, x_ref, y_ref,
):
    place = place_ref[0]
    width = base_ref.shape[0]
    shift = identity(width) * shift_ref[0]
    lead = coups_ref[3]
    lead_parts = split(lead)
    quarter = (
        dot_nt(lead_parts[0], lead_parts[0])
        + (dot_nt(lead_parts[0], lead_parts[1]) + dot_nt(lead_parts[1], lead_parts[0]))
    ) * 0.25
    last_ref[...] = diags_ref[3] - quarter

    def fill(pair, index, flipped):
        one, two = pair
        value = coups_ref[index]
        (two if flipped else one)[...] = value
        (one if flipped else two)[...] = value.T

    u, v, w, c = (u_ref, ut_ref), (v_ref, vt_ref), (w_ref, wt_ref), (c_ref, ct_ref)

    @pl.when(place == 0)
    def _():
        fill(u, 1, False)
        fill(v, 2, True)
        fill(w, 0, True)

    @pl.when(place == 1)
    def _():
        fill(c, 1, False)
        fill(v, 2, True)
        fill(w, 0, False)

    @pl.when(place == 2)
    def _():
        fill(c, 1, True)
        fill(v, 0, False)
        fill(w, 2, True)

    @pl.when(place == 3)
    def _():
        fill(u, 1, True)
        fill(v, 0, False)
        fill(w, 2, False)

    first = jnp.where(place == 0, 1, jnp.where(place == 1, 0, jnp.where(place == 2, 3, 2)))
    second = jnp.where(place <= 1, 3, 0)
    middle = jnp.where(place <= 1, 2, 1)

    def system(block):
        return jnp.where(block == 3, last_ref[...], diags_ref[block]) + shift

    inner = jnp.logical_or(place == 1, place == 2)
    invert([system(first), system(second)], [x_ref, y_ref])
    x = split(x_ref[...])
    y = split(y_ref[...])
    w_s, wt_s = split(w_ref[...]), split(wt_ref[...])
    xw = split(mul(x, w_s))
    yv = split(mul(y, split(v_ref[...])))
    rest = system(place) - mul(wt_s, xw)
    reduced_ref[...] = rest
    last_ref[...] = system(middle) - mul(split(vt_ref[...]), yv)

    @pl.when(jnp.logical_not(inner))
    def _():
        xu = split(mul(x, split(u_ref[...])))
        ut_s = split(ut_ref[...])
        last_ref[...] = last_ref[...] - mul(ut_s, xu)
        c_ref[...] = mul(wt_s, xu)
        ct_ref[...] = mul(ut_s, xw)

    invert([last_ref[...]], [x_ref])
    cz = split(product(c_ref[...], x_ref[...]))
    reduced = reduced_ref[...] - mul(cz, split(ct_ref[...]))
    reduced_ref[...] = reduced
    invert([reduced], [base_ref])


def screen(samples, bare, scale):
    count = len(samples)
    result = []
    for lag in range(count):
        total = samples[0] * samples[lag]
        for m in range(1, count - lag):
            total = total + samples[m] * samples[m + lag]
        scaled = bare * (total * scale)
        result.append(bare / jnp.sqrt(1.0 + scaled * scaled))
    return result


def regroup_kernel(
    count, base_ref, rows_ref, slots_ref, bare_pos_ref, spread_ref, taken_ref,
    lhs, arrived, selfen, taken, send_a, recv_a, send_b, recv_b, send_c, recv_c,
):
    me = lax.axis_index("energy")
    width = base_ref.shape[0]
    half = width // 2
    chunk = rows_ref.shape[2]
    lines = taken.shape[1]

    barrier = pltpu.get_barrier_semaphore()
    greet_energy(count, me, barrier)
    pl.semaphore_wait(barrier, count - 1)

    source_a = lambda peer: base_ref.at[pl.ds(pl.multiple_of(peer * 8, 8), 8), :]
    target_a = lambda peer: arrived.at[peer]
    send_blocks(count, me, source_a, target_a, send_a, recv_a)
    arrived[me] = base_ref[pl.ds(pl.multiple_of(me * 8, 8), 8), :]

    upper = base_ref[:half, :half]
    lower = base_ref[half:, half:]
    r = lax.broadcasted_iota(jnp.int32, (half, half), 0)
    c = lax.broadcasted_iota(jnp.int32, (half, half), 1)
    table = jnp.concatenate([jnp.where(r <= c, upper, lower), base_ref[:half, half:]], axis=1)
    diagonal = jnp.sum(jnp.where(r == c, lower, 0.0), axis=0, keepdims=True)
    extra = jnp.concatenate([jnp.zeros((1, half), F32), diagonal], axis=1)
    first = lax.broadcasted_iota(jnp.int32, (16, width), 0) == 0
    table = jnp.concatenate([table, jnp.where(first, extra, 0.0)], axis=0)
    high, low = split(table)
    tall = table.shape[0]
    lhs[:tall, :] = high
    lhs[tall:, :] = low
    row_index = lax.broadcasted_iota(jnp.int32, (width, chunk), 0)
    slot_index = lax.broadcasted_iota(jnp.int32, (tall, chunk), 0)

    def take(part, carry):
        hot = jnp.where(row_index == rows_ref[part], 1.0, 0.0).astype(BF16)
        both = dot(lhs[...], hot)
        found = jnp.where(slot_index == slots_ref[part], both[:tall] + both[tall:], 0.0)
        line = jnp.sum(found, axis=0, keepdims=True)
        for piece in range(chunk // 128):
            taken[part, piece:piece + 1, :] = line[:, piece * 128:(piece + 1) * 128]
        taken[part, chunk // 128:, :] = jnp.zeros((lines - chunk // 128, 128), F32)
        return carry

    lax.fori_loop(0, count, take, 0)
    source_c = lambda peer: taken.at[peer]
    target_c = lambda peer: taken_ref.at[peer]
    send_blocks(count, me, source_c, target_c, send_c, recv_c)
    taken_ref[me] = taken[me]
    await_blocks(count, me, source_a, target_a, send_a, recv_a)

    scale = polar_coef * width / count
    for side in range(width // 128):
        cols = slice(side * 128, (side + 1) * 128)
        samples = [arrived[e, :, cols] for e in range(count)]
        screened = screen(samples, bare_pos_ref[:, cols], scale)
        for e in range(count):
            total = samples[e] * screened[0]
            for n in range(1, e + 1):
                total = total + samples[e - n] * screened[n]
            selfen[e, :, cols] = total * (sigma_coef / count)
    source_b = lambda peer: selfen.at[peer]
    target_b = lambda peer: spread_ref.at[pl.ds(pl.multiple_of(peer * 8, 8), 8), :]
    send_blocks(count, me, source_b, target_b, send_b, recv_b)
    spread_ref[pl.ds(pl.multiple_of(me * 8, 8), 8), :] = selfen[me]
    await_blocks(count, me, source_b, target_b, send_b, recv_b)
    await_blocks(count, me, source_c, target_c, send_c, recv_c)


def finish_kernel(reduced_ref, base_ref, spread_ref, taken_ref, bare_ref, green_ref, screened_ref, x_ref):
    count = taken_ref.shape[0]
    width = base_ref.shape[0]
    chunk = screened_ref.shape[2]
    spread = spread_ref[...]
    matrix = reduced_ref[...] - 0.5 * (spread + spread.T)
    base = base_ref[...]
    residual = identity(width) - product(matrix, base)
    x_ref[...] = base

    @pl.when(jnp.logical_not(jnp.sum(residual * residual) < 0.5))
    def _():
        x_ref[...] = cold_start(matrix)

    settle([matrix], [x_ref])
    green_ref[0, 0] = x_ref[...]
    scale = polar_coef * width / count
    for group in range(taken_ref.shape[1] // 8):
        lines = slice(group * 8, group * 8 + 8)
        samples = [taken_ref[e, lines, :] for e in range(count)]
        screened = screen(samples, bare_ref[lines, :], scale)
        for line in range(group * 8, min(group * 8 + 8, pl.cdiv(chunk, 128))):
            start = line * 128
            stop = min(start + 128, chunk)
            for n in range(count):
                at = line - group * 8
                screened_ref[n, :, start:stop] = screened[n][at:at + 1, :stop - start]


def on_device(count, spaces, ham_diag, ham_coup, energies, pattern, coulomb):
    width = ham_diag.shape[1]
    span = coulomb.shape[1]
    chunk = pl.cdiv(span, 128) * 128
    lines = pl.cdiv(chunk // 128, 8) * 8
    vmem = pl.BlockSpec(memory_space=pltpu.VMEM)
    smem = pl.BlockSpec(memory_space=pltpu.SMEM)
    square = jax.ShapeDtypeStruct((width, width), F32)
    place = lax.axis_index("space").astype(jnp.int32).reshape(1)
    padded_pattern = jnp.pad(pattern, ((0, 0), (0, chunk - span)))
    padded_bare = jnp.pad(coulomb, ((0, 0), (0, chunk - span)))

    diags, coups, rows, slots, bare_pos, bare_own = pl.pallas_call(
        functools.partial(collect_kernel, count, spaces),
        out_shape=(
            jax.ShapeDtypeStruct((spaces, width, width), F32),
            jax.ShapeDtypeStruct((spaces, width, width), F32),
            jax.ShapeDtypeStruct((count, 1, chunk), jnp.int32),
            jax.ShapeDtypeStruct((count, 1, chunk), jnp.int32),
            jax.ShapeDtypeStruct((8, width), F32),
            jax.ShapeDtypeStruct((lines, 128), F32),
        ),
        in_specs=[vmem] * 4,
        out_specs=(vmem,) * 6,
        scratch_shapes=[
            VMEM((count, 1, chunk), jnp.int32), VMEM((width, width), F32), VMEM((count, 8, width), F32),
            DMA((2,)), DMA((spaces, 2)), DMA((spaces, 2)), DMA((spaces, 2)), DMA((spaces, 2)),
            DMA((count,)), DMA((count,)),
        ],
        compiler_params=pltpu.CompilerParams(collective_id=0, has_side_effects=True),
        name="collect",
    )(ham_diag, ham_coup, padded_pattern, padded_bare)

    reduced, base = pl.pallas_call(
        chain_kernel,
        out_shape=(square, square),
        in_specs=[smem, smem, vmem, vmem],
        out_specs=(vmem, vmem),
        scratch_shapes=[VMEM((width, width), F32)] * 11,
        name="chain",
    )(place, energies, diags, coups)

    spread, taken = pl.pallas_call(
        functools.partial(regroup_kernel, count),
        out_shape=(square, jax.ShapeDtypeStruct((count, lines, 128), F32)),
        in_specs=[vmem] * 4,
        out_specs=(vmem, vmem),
        scratch_shapes=[
            VMEM((2 * (width // 2 + 16), width), BF16), VMEM((count, 8, width), F32),
            VMEM((count, 8, width), F32), VMEM((count, lines, 128), F32),
            DMA((count,)), DMA((count,)), DMA((count,)), DMA((count,)), DMA((count,)), DMA((count,)),
        ],
        compiler_params=pltpu.CompilerParams(collective_id=1, has_side_effects=True),
        name="regroup",
    )(base, rows, slots, bare_pos)

    return pl.pallas_call(
        finish_kernel,
        out_shape=(
            jax.ShapeDtypeStruct((1, 1, width, width), F32),
            jax.ShapeDtypeStruct((count, 1, span), F32),
        ),
        in_specs=[vmem] * 5,
        out_specs=(vmem, vmem),
        scratch_shapes=[VMEM((width, width), F32)],
        name="finish",
    )(reduced, base, spread, taken, bare_own)


def solution(mesh):
    count, spaces = mesh.shape["energy"], mesh.shape["space"]
    return jax.shard_map(
        functools.partial(on_device, count, spaces),
        mesh=mesh,
        in_specs=(
            P("space", None, None),
            P("space", None, None),
            P("energy"),
            P("space", None),
            P("space", "energy"),
        ),
        out_specs=(P("energy", "space", None, None), P(None, "space", "energy")),
        check_vma=False,
    )
```

time: 1700 us -> 78 us (0.05)
  local copies, waits for them, and re-layouts: 818 us -> 2.33 us
  other arithmetic: 788 us -> 0 us
  Pallas kernels: 0 us -> 74.1 us
  starting transfers between devices: 33.4 us -> 0 us
  matrix products: 27.9 us -> 0 us
    another operation x76 -> x0, other arithmetic: 457 us -> none  [the longest x20 180 us: tri_solve(): lax.linalg.triangular_solve(factor, target, left_side=True, lower=True, t...]
    unnamed x6 -> x0, other arithmetic: 326 us -> none
    all_to_all x2 -> x0, local copies, waits for them, and re-layouts: 324 us -> none  [the longest x1 324 us: on_device(): lax.all_to_all(samples, 'energy', split_axis=2, concat_axis=0, tiled=True)]
    gather x1 -> x0, local copies, waits for them, and re-layouts: 222 us -> none  [on_device(): samples = jnp.take_along_axis(flat, pattern[None], axis=2)]
    unnamed x15 -> x2, local copies, waits for them, and re-layouts: 202 us -> 0.02 us
    pallas_call x0 -> x4, Pallas kernels: none -> 74.1 us  [the longest x1 28.6 us: on_device(): pl.pallas_call(functools.partial(regroup_kernel, count), out_shape=(squar...]
    another operation x111 -> x0, local copies, waits for them, and re-layouts: 38.2 us -> none  [the longest x80 37.1 us: tri_solve(): lax.linalg.triangular_solve(factor, target, left_side=True, lower=True, t...]
    select_n x1 -> x0, local copies, waits for them, and re-layouts: 31.1 us -> none  [on_device(): samples = jnp.take_along_axis(flat, pattern[None], axis=2)]
  transfers between devices with their start and end apart: 8 -> 0, of which waited for: 2 -> 0; matrix products, arithmetic and copies ran while one was open for 16% -> 0% of each run, Pallas kernels for 0% -> 0%
where the time goes in v1:
time: 78 us; the launch traced here: 77.7 us
  Pallas kernels  74.1 us (95%)
  local copies, waits for them, and re-layouts  2.33 us (3%)
  between operations  1.31 us (2%)
    pallas_call x1, Pallas kernels, on_device(): pl.pallas_call(functools.partial(regroup_kernel, count), out_shape=(squar...  28.6 us
    pallas_call x1, Pallas kernels, on_device(): pl.pallas_call(functools.partial(collect_kernel, count, spaces), out_shap...  27.6 us
    pallas_call x1, Pallas kernels, on_device(): pl.pallas_call(chain_kernel, out_shape=(square, square), in_specs=[smem,...  14.1 us
    pallas_call x1, Pallas kernels, on_device(): pl.pallas_call(finish_kernel, out_shape=(jax.ShapeDtypeStruct((1, 1, widt...  3.8 us
    pad x1, local copies, waits for them, and re-layouts, on_device(): padded_pattern = jnp.pad(pattern, ((0, 0), (0, chunk - span)))  1.71 us

profile of v1, /device:TPU:1, one launch (start us, length us, event | category | flops | bytes accessed | tf_op | source)
XLA Modules:
  0.0 77.7 jit_solution(15945074475766260806)
XLA Ops:
  0.6 0.0 copy-start
  1.3 0.0 copy-done
  1.3 0.6 pad.9.bare_ref
  1.9 1.7 %pad.8.pattern_ref = s32[1,43320]{1,0:T(1,128)} pad(s32[1,43264]{1,0:T(1,128)} %param.8, s32[]{:T(128)} %constant.6.clone.1), padding=0_0x0_56 | pad | bytes 346340 | tf_op jit(solution)/shard_map/jit(_pad)/pad | solution.py:458
  3.6 27.6 %collect.1 = (f32[4,256,256]{2,1,0:T(8,128)}, f32[4,256,256]{2,1,0:T(8,128)}, s32[32,1,1408]{2,1,0:T(1,128)}, s32[32,1,1408]{2,1,0:T(1,128)}, f32[8,256]{1,0:T(8,128)}, /*index=5*/f32[16,128]{1,0:T(8,128)}) custom-call(f32[1,256,256]{2,1,0:T(8,128)} %diag_ref.1, f32[1,256,256]{2,1,0:T(8,128)} %coup_ref.1, s32[1,43320]{1,0:T(1,128)} %pad.8.pattern_ref, ...), custom_call_target="tpu_custom_call" | custom-call | tf_op jit(solution)/shard_map/collect/pallas_call | solution.py:461
  31.3 14.1 %chain.1 = (f32[256,256]{1,0:T(8,128)}, f32[256,256]{1,0:T(8,128)}) custom-call(s32[1]{0:T(128)} %bitcast.place_ref, f32[1]{0:T(128)S(6)} %copy.7.shift_ref, f32[4,256,256]{2,1,0:T(8,128)} %get-tuple-element.12.diags_ref, f32[4,256,256]{2,1,0:T(8,128)} %get-tuple-element.13.coups_ref), custom_call_target="tpu_custom_call" | custom-call | tf_op jit(solution)/shard_map/chain/pallas_call | solution.py:482
  45.3 28.6 %regroup.1 = (f32[256,256]{1,0:T(8,128)}, f32[32,16,128]{2,1,0:T(8,128)}) custom-call(f32[256,256]{1,0:T(8,128)} %get-tuple-element.15.base_ref, s32[32,1,1408]{2,1,0:T(1,128)} %get-tuple-element.16.rows_ref, s32[32,1,1408]{2,1,0:T(1,128)} %get-tuple-element.17.slots_ref, f32[8,256]{1,0:T(8,128)} %get-tuple-element.18.bare_pos_ref), custom_call_target="tpu_custom_call" | custom-call | tf_op jit(solution)/shard_map/regroup/pallas_call | solution.py:491
  73.9 3.8 %finish.1 = (f32[1,1,256,256]{3,2,1,0:T(8,128)}, f32[32,1,1352]{2,1,0:T(1,128)}) custom-call(f32[256,256]{1,0:T(8,128)} %get-tuple-element.14.reduced_ref, f32[256,256]{1,0:T(8,128)} %get-tuple-element.15.base_ref, f32[256,256]{1,0:T(8,128)} %get-tuple-element.19.spread_ref, f32[32,16,128]{2,1,0:T(8,128)} %get-tuple-element.20.taken_ref, ...), custom_call_target="tpu_custom_call" | custom-call | tf_op jit(solution)/shard_map/finish/pallas_call | solution.py:505
Async XLA Ops:
  0.6 0.7 copy-start

commit v2 on v1

--- a/solution.py
+++ b/solution.py
@@ -111,14 +111,25 @@
     settle(matrices, refs)
 
 
+def peer_of(me, offset):
+    core = lax.rem(me + offset, 2)
+    y = lax.rem(me // 2 + offset // 2, 4)
+    z = lax.rem(me // 8 + offset // 8, 4)
+    return z * 8 + y * 2 + core
+
+
+def block_copy(me, offset, source, target, slot, send_sems, recv_sems):
+    peer = peer_of(me, offset)
+    return pltpu.make_async_remote_copy(
+        src_ref=source(peer), dst_ref=target(slot),
+        send_sem=send_sems.at[offset], recv_sem=recv_sems.at[slot],
+        device_id={"energy": peer}, device_id_type=MESH,
+    )
+
+
 def send_blocks(count, me, source, target, send_sems, recv_sems):
     def one(step, carry):
-        peer = lax.rem(me + step, count)
-        pltpu.make_async_remote_copy(
-            src_ref=source(peer), dst_ref=target(me),
-            send_sem=send_sems.at[step], recv_sem=recv_sems.at[me],
-            device_id={"energy": peer}, device_id_type=MESH,
-        ).start()
+        block_copy(me, count - step, source, target, me, send_sems, recv_sems).start()
         return carry
 
     lax.fori_loop(1, count, one, 0)
@@ -126,12 +137,8 @@
 
 def await_blocks(count, me, source, target, send_sems, recv_sems):
     def one(step, carry):
-        peer = lax.rem(me + step, count)
-        copy = pltpu.make_async_remote_copy(
-            src_ref=source(peer), dst_ref=target(peer),
-            send_sem=send_sems.at[step], recv_sem=recv_sems.at[peer],
-            device_id={"energy": peer}, device_id_type=MESH,
-        )
+        offset = count - step
+        copy = block_copy(me, offset, source, target, peer_of(me, offset), send_sems, recv_sems)
         copy.wait_send()
         copy.wait_recv()
         return carry
@@ -139,18 +146,14 @@
     lax.fori_loop(1, count, one, 0)
 
 
-def greet_energy(count, me, barrier):
-    def one(step, carry):
-        pl.semaphore_signal(barrier, inc=1, device_id={"energy": lax.rem(me + step, count)}, device_id_type=MESH)
-        return carry
-
-    lax.fori_loop(1, count, one, 0)
+def rows_of(ref, peer):
+    return ref.at[pl.ds(pl.multiple_of(peer * 8, 8), 8), :]
 
 
 def collect_kernel(
     count, spaces, diag_ref, coup_ref, pattern_ref, bare_ref,
-    diags_ref, coups_ref, rows_ref, slots_ref, bare_pos_ref, bare_own_ref,
-    own_pattern, partial, arrived, own_sem, far_send, far_recv, near_send, near_recv, send_sems, recv_sems,
+    diags_ref, coups_ref, rows_ref, slots_ref, partial_ref, bare_own_ref,
+    own_pattern, own_bare, own_sem, far_send, far_recv, near_send, near_recv,
 ):
     me = lax.axis_index("energy")
     place = lax.axis_index("space")
@@ -158,38 +161,43 @@
     half = width // 2
     core = lax.rem(me, 2)
     other = me + 1 - 2 * core
-    chunk = bare_ref.shape[1]
-    span = 1352
+    span = bare_ref.shape[1]
+    chunk = own_bare.shape[1]
+    sides = (lax.rem(place + 1, spaces), lax.rem(place + spaces - 1, spaces))
+    across = lax.rem(place + 2, spaces)
 
     barrier = pltpu.get_barrier_semaphore()
-    greet_energy(count, me, barrier)
-    for step in range(1, spaces):
-        pl.semaphore_signal(
-            barrier, inc=1, device_id={"space": lax.rem(place + step, spaces)}, device_id_type=MESH)
-    pl.semaphore_wait(barrier, count + spaces - 2)
+    for side in sides:
+        pl.semaphore_signal(barrier, inc=1, device_id={"space": side}, device_id_type=MESH)
+    pl.semaphore_signal(barrier, inc=1, device_id={"energy": other}, device_id_type=MESH)
+    pl.semaphore_wait(barrier, 3)
 
     own_half = pl.ds(pl.multiple_of(core * half, half), half)
     other_half = pl.ds(pl.multiple_of((1 - core) * half, half), half)
-
-    def far_copy(step, kind):
-        source, store = ((diag_ref, diags_ref), (coup_ref, coups_ref))[kind]
+    given = (diag_ref, coup_ref)
+    stores = (diags_ref, coups_ref)
+
+    def far(way, stage):
+        kind = (way, 1 - way, way)[stage]
+        block = place if stage < 2 else sides[1 - way]
+        source = given[kind].at[0, own_half] if stage < 2 else stores[kind].at[block, own_half]
         return pltpu.make_async_remote_copy(
-            src_ref=source.at[0, own_half], dst_ref=store.at[place, own_half],
-            send_sem=far_send.at[step, kind], recv_sem=far_recv.at[step, kind],
-            device_id={"space": lax.rem(place + step, spaces)}, device_id_type=MESH)
-
-    def near_copy(step, kind):
-        store = (diags_ref, coups_ref)[kind]
-        source = lax.rem(place + spaces - step, spaces)
+            src_ref=source, dst_ref=stores[kind].at[block, own_half],
+            send_sem=far_send.at[way, stage], recv_sem=far_recv.at[way, stage],
+            device_id={"space": sides[way]}, device_id_type=MESH)
+
+    def near(way, stage, part):
+        kind = (way, 1 - way, way)[stage]
+        block = sides[1 - way] if stage < 2 else across
+        piece = stores[kind].at[block, part]
         return pltpu.make_async_remote_copy(
-            src_ref=store.at[source, own_half], dst_ref=store.at[source, own_half],
-            send_sem=near_send.at[step, kind], recv_sem=near_recv.at[step, kind],
+            src_ref=piece, dst_ref=piece,
+            send_sem=near_send.at[way, stage], recv_sem=near_recv.at[way, stage],
             device_id={"energy": other}, device_id_type=MESH)
 
-    order = (1, 3, 2)
-    for step in order:
-        for kind in range(2):
-            far_copy(step, kind).start()
+    for stage in range(2):
+        for way in range(2):
+            far(way, stage).start()
     own_copies = [
         pltpu.make_async_copy(diag_ref.at[0], diags_ref.at[place], own_sem.at[0]),
         pltpu.make_async_copy(coup_ref.at[0], coups_ref.at[place], own_sem.at[1]),
@@ -197,19 +205,33 @@
     for copy in own_copies:
         copy.start()
 
+    tail = chunk - 128
     for part in range(count):
-        piece = pattern_ref[:, part * span:part * span + chunk]
-        own_pattern[part] = piece
+        size = chunk if part < count - 1 else span
+        if size < chunk:
+            own_pattern[part, :, tail:] = jnp.zeros((1, 128), jnp.int32)
+            rows_ref[part, :, tail:] = jnp.zeros((1, 128), jnp.int32)
+            slots_ref[part, :, tail:] = jnp.zeros((1, 128), jnp.int32)
+        piece = pattern_ref[:, part * span:part * span + size]
+        own_pattern[part, :, :size] = piece
         row = lax.shift_right_logical(piece, 8)
         col = jnp.bitwise_and(piece, 255)
         high = jnp.maximum(row, col)
         low = jnp.minimum(row, col)
         lower = low >= 128
         pivot = high == low
-        rows_ref[part] = jnp.where(jnp.logical_and(lower, jnp.logical_not(pivot)), low - 128, high)
-        slots_ref[part] = jnp.where(lower, jnp.where(pivot, 128, high - 128), low)
+        rows_ref[part, :, :size] = jnp.where(jnp.logical_and(lower, jnp.logical_not(pivot)), low - 128, high)
+        slots_ref[part, :, :size] = jnp.where(lower, jnp.where(pivot, 128, high - 128), low)
+    own_bare[:, tail:] = jnp.zeros((1, 128), F32)
+    own_bare[:, :span] = bare_ref[...]
+
+    for way in range(2):
+        far(way, 0).wait_recv()
+        far(way, 2).start()
+        near(way, 0, own_half).start()
+
     mine = own_pattern[me]
-    bare = bare_ref[...]
+    bare = own_bare[...]
     index = lax.broadcasted_iota(jnp.int32, (width, chunk), 0)
     on_row = index == lax.shift_right_logical(mine, 8)
     on_col = jnp.where(index == jnp.bitwise_and(mine, 255), 1.0, 0.0).astype(BF16)
@@ -220,46 +242,30 @@
         rest = rest - part
         term = dot_nt(jnp.where(on_row, part, 0.0).astype(BF16), on_col)
         total = term if total is None else total + term
-    partial[...] = total
+    partial_ref[...] = total
     for line in range(chunk // 128):
         bare_own_ref[line:line + 1, :] = bare[:, line * 128:(line + 1) * 128]
     for line in range(chunk // 128, bare_own_ref.shape[0]):
         bare_own_ref[line:line + 1, :] = jnp.zeros((1, 128), F32)
 
-    source = lambda peer: partial.at[pl.ds(pl.multiple_of(peer * 8, 8), 8), :]
-    target = lambda peer: arrived.at[peer]
-    send_blocks(count, me, source, target, send_sems, recv_sems)
-    arrived[me] = partial[pl.ds(pl.multiple_of(me * 8, 8), 8), :]
-
-    for step in order:
-        for kind in range(2):
-            copy = far_copy(step, kind)
-            copy.wait_recv()
-            near_copy(step, kind).start()
-    await_blocks(count, me, source, target, send_sems, recv_sems)
-    pieces = [arrived[peer] for peer in range(count)]
-    while len(pieces) > 1:
-        pieces = [pieces[i] + pieces[i + 1] for i in range(0, len(pieces), 2)]
-    bare_pos_ref[...] = pieces[0]
+    for stage in (1, 2):
+        for way in range(2):
+            far(way, stage).wait_recv()
+            near(way, stage, own_half).start()
     for copy in own_copies:
         copy.wait()
-    for step in order:
-        for kind in range(2):
-            far_copy(step, kind).wait_send()
-            near_copy(step, kind).wait_send()
-            store = (diags_ref, coups_ref)[kind]
-            block = lax.rem(place + spaces - step, spaces)
-            pltpu.make_async_remote_copy(
-                src_ref=store.at[block, other_half], dst_ref=store.at[block, other_half],
-                send_sem=near_send.at[step, kind], recv_sem=near_recv.at[step, kind],
-                device_id={"energy": other}, device_id_type=MESH).wait_recv()
+    for stage in range(3):
+        for way in range(2):
+            far(way, stage).wait_send()
+            near(way, stage, own_half).wait_send()
+            near(way, stage, other_half).wait_recv()
 
 
 def chain_kernel(
-    place_ref, shift_ref, diags_ref, coups_ref, reduced_ref, base_ref,
+    shift_ref, diags_ref, coups_ref, reduced_ref, base_ref,
     u_ref, ut_ref, v_ref, vt_ref, w_ref, wt_ref, c_ref, ct_ref, last_ref, x_ref, y_ref,
 ):
-    place = place_ref[0]
+    place = lax.axis_index("space")
     width = base_ref.shape[0]
     shift = identity(width) * shift_ref[0]
     lead = coups_ref[3]
@@ -347,9 +353,14 @@
     return result
 
 
+TAKEN_FIRST = 4
+TAKEN_SECOND = 13
+
+
 def regroup_kernel(
-    count, base_ref, rows_ref, slots_ref, bare_pos_ref, spread_ref, taken_ref,
-    lhs, arrived, selfen, taken, send_a, recv_a, send_b, recv_b, send_c, recv_c,
+    count, base_ref, partial_ref, rows_ref, slots_ref, spread_ref, taken_ref,
+    lhs, arrived, bares, selfen, taken,
+    send_a, recv_a, send_b, recv_b, send_c, recv_c, send_d, recv_d,
 ):
     me = lax.axis_index("energy")
     width = base_ref.shape[0]
@@ -358,13 +369,13 @@
     lines = taken.shape[1]
 
     barrier = pltpu.get_barrier_semaphore()
-    greet_energy(count, me, barrier)
-    pl.semaphore_wait(barrier, count - 1)
-
-    source_a = lambda peer: base_ref.at[pl.ds(pl.multiple_of(peer * 8, 8), 8), :]
-    target_a = lambda peer: arrived.at[peer]
-    send_blocks(count, me, source_a, target_a, send_a, recv_a)
-    arrived[me] = base_ref[pl.ds(pl.multiple_of(me * 8, 8), 8), :]
+
+    def greet(step, carry):
+        pl.semaphore_signal(
+            barrier, inc=1, device_id={"energy": peer_of(me, count - step)}, device_id_type=MESH)
+        return carry
+
+    lax.fori_loop(1, count, greet, 0)
 
     upper = base_ref[:half, :half]
     lower = base_ref[half:, half:]
@@ -377,41 +388,66 @@
     table = jnp.concatenate([table, jnp.where(first, extra, 0.0)], axis=0)
     high, low = split(table)
     tall = table.shape[0]
+    used = half + 8
     lhs[:tall, :] = high
     lhs[tall:, :] = low
     row_index = lax.broadcasted_iota(jnp.int32, (width, chunk), 0)
-    slot_index = lax.broadcasted_iota(jnp.int32, (tall, chunk), 0)
-
-    def take(part, carry):
+    slot_index = lax.broadcasted_iota(jnp.int32, (used, chunk), 0)
+
+    def take(part):
         hot = jnp.where(row_index == rows_ref[part], 1.0, 0.0).astype(BF16)
         both = dot(lhs[...], hot)
-        found = jnp.where(slot_index == slots_ref[part], both[:tall] + both[tall:], 0.0)
+        found = jnp.where(slot_index == slots_ref[part], both[:used] + both[tall:tall + used], 0.0)
         line = jnp.sum(found, axis=0, keepdims=True)
         for piece in range(chunk // 128):
             taken[part, piece:piece + 1, :] = line[:, piece * 128:(piece + 1) * 128]
         taken[part, chunk // 128:, :] = jnp.zeros((lines - chunk // 128, 128), F32)
+
+    source_a, target_a = lambda peer: rows_of(base_ref, peer), lambda slot: arrived.at[slot]
+    source_d, target_d = lambda peer: rows_of(partial_ref, peer), lambda slot: bares.at[slot]
+    source_b, target_b = lambda peer: selfen.at[peer], lambda slot: rows_of(spread_ref, slot)
+    source_c, target_c = lambda peer: taken.at[peer], lambda slot: taken_ref.at[slot]
+
+    def take_only(step, carry):
+        take(peer_of(me, count - step))
         return carry
 
-    lax.fori_loop(0, count, take, 0)
-    source_c = lambda peer: taken.at[peer]
-    target_c = lambda peer: taken_ref.at[peer]
-    send_blocks(count, me, source_c, target_c, send_c, recv_c)
-    taken_ref[me] = taken[me]
+    def send_only(step, carry):
+        block_copy(me, count - step, source_c, target_c, me, send_c, recv_c).start()
+        return carry
+
+    def take_and_send(step, carry):
+        take_only(step, carry)
+        return send_only(step, carry)
+
+    lax.fori_loop(1, 1 + TAKEN_FIRST, take_only, 0)
+    pl.semaphore_wait(barrier, count - 1)
+    send_blocks(count, me, source_a, target_a, send_a, recv_a)
+    send_blocks(count, me, source_d, target_d, send_d, recv_d)
+    lax.fori_loop(1, 1 + TAKEN_FIRST, send_only, 0)
+    arrived[me] = rows_of(base_ref, me)[...]
+    bares[me] = rows_of(partial_ref, me)[...]
+    lax.fori_loop(1 + TAKEN_FIRST, 1 + TAKEN_FIRST + TAKEN_SECOND, take_and_send, 0)
     await_blocks(count, me, source_a, target_a, send_a, recv_a)
+    await_blocks(count, me, source_d, target_d, send_d, recv_d)
 
     scale = polar_coef * width / count
     for side in range(width // 128):
         cols = slice(side * 128, (side + 1) * 128)
+        bare = bares[0, :, cols]
+        for e in range(1, count):
+            bare = bare + bares[e, :, cols]
         samples = [arrived[e, :, cols] for e in range(count)]
-        screened = screen(samples, bare_pos_ref[:, cols], scale)
+        screened = screen(samples, bare, scale)
         for e in range(count):
             total = samples[e] * screened[0]
             for n in range(1, e + 1):
                 total = total + samples[e - n] * screened[n]
             selfen[e, :, cols] = total * (sigma_coef / count)
-    source_b = lambda peer: selfen.at[peer]
-    target_b = lambda peer: spread_ref.at[pl.ds(pl.multiple_of(peer * 8, 8), 8), :]
     send_blocks(count, me, source_b, target_b, send_b, recv_b)
+    lax.fori_loop(1 + TAKEN_FIRST + TAKEN_SECOND, count, take_and_send, 0)
+    take(me)
+    taken_ref[me] = taken[me]
     spread_ref[pl.ds(pl.multiple_of(me * 8, 8), 8), :] = selfen[me]
     await_blocks(count, me, source_b, target_b, send_b, recv_b)
     await_blocks(count, me, source_c, target_c, send_c, recv_c)
@@ -454,39 +490,34 @@
     vmem = pl.BlockSpec(memory_space=pltpu.VMEM)
     smem = pl.BlockSpec(memory_space=pltpu.SMEM)
     square = jax.ShapeDtypeStruct((width, width), F32)
-    place = lax.axis_index("space").astype(jnp.int32).reshape(1)
-    padded_pattern = jnp.pad(pattern, ((0, 0), (0, chunk - span)))
-    padded_bare = jnp.pad(coulomb, ((0, 0), (0, chunk - span)))
-
-    diags, coups, rows, slots, bare_pos, bare_own = pl.pallas_call(
+    diags, coups, rows, slots, partial, bare_own = pl.pallas_call(
         functools.partial(collect_kernel, count, spaces),
         out_shape=(
             jax.ShapeDtypeStruct((spaces, width, width), F32),
             jax.ShapeDtypeStruct((spaces, width, width), F32),
             jax.ShapeDtypeStruct((count, 1, chunk), jnp.int32),
             jax.ShapeDtypeStruct((count, 1, chunk), jnp.int32),
-            jax.ShapeDtypeStruct((8, width), F32),
+            square,
             jax.ShapeDtypeStruct((lines, 128), F32),
         ),
         in_specs=[vmem] * 4,
         out_specs=(vmem,) * 6,
         scratch_shapes=[
-            VMEM((count, 1, chunk), jnp.int32), VMEM((width, width), F32), VMEM((count, 8, width), F32),
-            DMA((2,)), DMA((spaces, 2)), DMA((spaces, 2)), DMA((spaces, 2)), DMA((spaces, 2)),
-            DMA((count,)), DMA((count,)),
+            VMEM((count, 1, chunk), jnp.int32), VMEM((1, chunk), F32),
+            DMA((2,)), DMA((2, 3)), DMA((2, 3)), DMA((2, 3)), DMA((2, 3)),
         ],
         compiler_params=pltpu.CompilerParams(collective_id=0, has_side_effects=True),
         name="collect",
-    )(ham_diag, ham_coup, padded_pattern, padded_bare)
+    )(ham_diag, ham_coup, pattern, coulomb)
 
     reduced, base = pl.pallas_call(
         chain_kernel,
         out_shape=(square, square),
-        in_specs=[smem, smem, vmem, vmem],
+        in_specs=[smem, vmem, vmem],
         out_specs=(vmem, vmem),
         scratch_shapes=[VMEM((width, width), F32)] * 11,
         name="chain",
-    )(place, energies, diags, coups)
+    )(energies, diags, coups)
 
     spread, taken = pl.pallas_call(
         functools.partial(regroup_kernel, count),
@@ -495,12 +526,11 @@
         out_specs=(vmem, vmem),
         scratch_shapes=[
             VMEM((2 * (width // 2 + 16), width), BF16), VMEM((count, 8, width), F32),
-            VMEM((count, 8, width), F32), VMEM((count, lines, 128), F32),
-            DMA((count,)), DMA((count,)), DMA((count,)), DMA((count,)), DMA((count,)), DMA((count,)),
-        ],
+            VMEM((count, 8, width), F32), VMEM((count, 8, width), F32), VMEM((count, lines, 128), F32),
+        ] + [DMA((count,))] * 8,
         compiler_params=pltpu.CompilerParams(collective_id=1, has_side_effects=True),
         name="regroup",
-    )(base, rows, slots, bare_pos)
+    )(base, partial, rows, slots)
 
     return pl.pallas_call(
         finish_kernel,

time: 78 us -> 66.8 us (0.86)
  Pallas kernels: 74.1 us -> 65.3 us
  local copies, waits for them, and re-layouts: 2.33 us -> 0 us
    pallas_call x1, Pallas kernels: 27.6 us -> 18 us  [on_device(): pl.pallas_call(functools.partial(collect_kernel, count, spaces), out_shap...]
    pad x2 -> x0, local copies, waits for them, and re-layouts: 2.31 us -> none  [the longest x1 1.71 us: on_device(): padded_pattern = jnp.pad(pattern, ((0, 0), (0, chunk - span)))]
    pallas_call x1, Pallas kernels: 28.6 us -> 29.5 us  [on_device(): pl.pallas_call(functools.partial(regroup_kernel, count), out_shape=(squar...]
where the time goes in v2:
time: 66.8 us; the launch traced here: 66.6 us
  Pallas kernels  65.3 us (98%)
  between operations  1.29 us (2%)
    pallas_call x1, Pallas kernels, on_device(): pl.pallas_call(functools.partial(regroup_kernel, count), out_shape=(squar...  29.5 us
    pallas_call x1, Pallas kernels, on_device(): pl.pallas_call(functools.partial(collect_kernel, count, spaces), out_shap...  18 us
    pallas_call x1, Pallas kernels, on_device(): pl.pallas_call(chain_kernel, out_shape=(square, square), in_specs=[smem,...  14 us
    pallas_call x1, Pallas kernels, on_device(): pl.pallas_call(finish_kernel, out_shape=(jax.ShapeDtypeStruct((1, 1, widt...  3.8 us

profile of v2, /device:TPU:1, one launch (start us, length us, event | category | flops | bytes accessed | tf_op | source)
XLA Modules:
  0.0 66.6 jit_solution(13920632357700605310)
XLA Ops:
  1.3 18.0 %collect.1 = (f32[4,256,256]{2,1,0:T(8,128)}, f32[4,256,256]{2,1,0:T(8,128)}, s32[32,1,1408]{2,1,0:T(1,128)}, s32[32,1,1408]{2,1,0:T(1,128)}, f32[256,256]{1,0:T(8,128)}, /*index=5*/f32[16,128]{1,0:T(8,128)}) custom-call(f32[1,256,256]{2,1,0:T(8,128)} %diag_ref.1, f32[1,256,256]{2,1,0:T(8,128)} %coup_ref.1, s32[1,43264]{1,0:T(1,128)} %pattern_ref.1, ...), custom_call_target="tpu_custom_call" | custom-call | tf_op jit(solution)/shard_map/collect/pallas_call | solution.py:493
  19.3 14.0 %chain.1 = (f32[256,256]{1,0:T(8,128)}, f32[256,256]{1,0:T(8,128)}) custom-call(f32[1]{0:T(128)S(6)} %copy.7.shift_ref, f32[4,256,256]{2,1,0:T(8,128)} %get-tuple-element.12.diags_ref, f32[4,256,256]{2,1,0:T(8,128)} %get-tuple-element.13.coups_ref), custom_call_target="tpu_custom_call" | custom-call | tf_op jit(solution)/shard_map/chain/pallas_call | solution.py:513
  33.3 29.5 %regroup.1 = (f32[256,256]{1,0:T(8,128)}, f32[32,16,128]{2,1,0:T(8,128)}) custom-call(f32[256,256]{1,0:T(8,128)} %get-tuple-element.15.base_ref, f32[256,256]{1,0:T(8,128)} %get-tuple-element.16.partial_ref, s32[32,1,1408]{2,1,0:T(1,128)} %get-tuple-element.17.rows_ref, s32[32,1,1408]{2,1,0:T(1,128)} %get-tuple-element.18.slots_ref), custom_call_target="tpu_custom_call" | custom-call | tf_op jit(solution)/shard_map/regroup/pallas_call | solution.py:522
  62.8 3.8 %finish.1 = (f32[1,1,256,256]{3,2,1,0:T(8,128)}, f32[32,1,1352]{2,1,0:T(1,128)}) custom-call(f32[256,256]{1,0:T(8,128)} %get-tuple-element.14.reduced_ref, f32[256,256]{1,0:T(8,128)} %get-tuple-element.15.base_ref, f32[256,256]{1,0:T(8,128)} %get-tuple-element.19.spread_ref, f32[32,16,128]{2,1,0:T(8,128)} %get-tuple-element.20.taken_ref, ...), custom_call_target="tpu_custom_call" | custom-call | tf_op jit(solution)/shard_map/finish/pallas_call | solution.py:535

commit v3 on v2

--- a/solution.py
+++ b/solution.py
@@ -15,9 +15,8 @@
 polar_coef = 128.0
 sigma_coef = 0.5
 
-START_DOUBLINGS = 5
-MAX_STEPS = 48
 TOLERANCE = 1e-6
+VMEM_LIMIT = 20 << 20
 
 
 def split(value):
@@ -47,17 +46,27 @@
     return jnp.where(rows == cols, 1.0, 0.0).astype(F32)
 
 
-def cold_start(matrix):
-    ident = identity(matrix.shape[0])
-    bound = jnp.max(jnp.sum(jnp.abs(matrix), axis=0, keepdims=True), axis=1, keepdims=True)
-    alpha = 1.9 / bound
-    power = ident - matrix * alpha
-    guess = (ident + power) * alpha
-    for _ in range(START_DOUBLINGS):
+def series(matrix, alpha, doublings):
+    power = identity(matrix.shape[0]) - matrix * alpha
+    guess = alpha * (identity(matrix.shape[0]) + power)
+    for _ in range(doublings):
         high = power.astype(BF16)
         power = dot(high, high)
         guess = guess + dot(guess.astype(BF16), power.astype(BF16))
     return guess
+
+
+def total_of(value):
+    return jnp.sum(jnp.sum(value, axis=0, keepdims=True), axis=1, keepdims=True)
+
+
+def mean_scale(matrix):
+    trace = total_of(jnp.where(identity(matrix.shape[0]) > 0.0, matrix, 0.0))
+    return trace / total_of(matrix * matrix)
+
+
+def safe_scale(matrix):
+    return 1.9 / jnp.max(jnp.sum(jnp.abs(matrix), axis=0, keepdims=True), axis=1, keepdims=True)
 
 
 def eliminate(matrix, out_ref):
@@ -79,13 +88,13 @@
     lax.fori_loop(0, width, step, 0)
 
 
-def settle(matrices, refs):
+def newton(matrices, refs, limit):
     ident = identity(matrices[0].shape[0])
     parts = [split(matrix) for matrix in matrices]
 
     def unsettled(carry):
         steps, worst = carry
-        return jnp.logical_and(worst > TOLERANCE, steps < MAX_STEPS)
+        return jnp.logical_and(worst > TOLERANCE, steps < limit)
 
     def step(carry):
         worst = jnp.float32(0.0)
@@ -97,17 +106,27 @@
             worst = jnp.maximum(worst, jnp.sum(residual * residual))
         return carry[0] + 1, worst
 
-    steps, worst = lax.while_loop(unsettled, step, (jnp.int32(0), jnp.float32(1.0)))
+    return lax.while_loop(unsettled, step, (jnp.int32(0), jnp.float32(1.0)))[1]
+
+
+def settle(matrices, refs):
+    worst = newton(matrices, refs, 8)
 
     @pl.when(jnp.logical_not(worst <= TOLERANCE))
     def _():
         for matrix, ref in zip(matrices, refs):
-            eliminate(matrix, ref)
+            ref[...] = series(matrix, safe_scale(matrix), 5)
+        again = newton(matrices, refs, 48)
+
+        @pl.when(jnp.logical_not(again <= TOLERANCE))
+        def _():
+            for matrix, ref in zip(matrices, refs):
+                eliminate(matrix, ref)
 
 
 def invert(matrices, refs):
     for matrix, ref in zip(matrices, refs):
-        ref[...] = cold_start(matrix)
+        ref[...] = series(matrix, mean_scale(matrix), 3)
     settle(matrices, refs)
 
 
@@ -263,73 +282,48 @@
 
 def chain_kernel(
     shift_ref, diags_ref, coups_ref, reduced_ref, base_ref,
-    u_ref, ut_ref, v_ref, vt_ref, w_ref, wt_ref, c_ref, ct_ref, last_ref, x_ref, y_ref,
+    v_ref, vt_ref, w_ref, wt_ref, c_ref, ct_ref, last_ref, x_ref, y_ref,
 ):
     place = lax.axis_index("space")
     width = base_ref.shape[0]
     shift = identity(width) * shift_ref[0]
-    lead = coups_ref[3]
-    lead_parts = split(lead)
+    lead_parts = split(coups_ref[3])
     quarter = (
         dot_nt(lead_parts[0], lead_parts[0])
         + (dot_nt(lead_parts[0], lead_parts[1]) + dot_nt(lead_parts[1], lead_parts[0]))
     ) * 0.25
     last_ref[...] = diags_ref[3] - quarter
-
-    def fill(pair, index, flipped):
-        one, two = pair
-        value = coups_ref[index]
-        (two if flipped else one)[...] = value
-        (one if flipped else two)[...] = value.T
-
-    u, v, w, c = (u_ref, ut_ref), (v_ref, vt_ref), (w_ref, wt_ref), (c_ref, ct_ref)
-
-    @pl.when(place == 0)
-    def _():
-        fill(u, 1, False)
-        fill(v, 2, True)
-        fill(w, 0, True)
-
-    @pl.when(place == 1)
-    def _():
-        fill(c, 1, False)
-        fill(v, 2, True)
-        fill(w, 0, False)
-
-    @pl.when(place == 2)
-    def _():
-        fill(c, 1, True)
-        fill(v, 0, False)
-        fill(w, 2, True)
-
-    @pl.when(place == 3)
-    def _():
-        fill(u, 1, True)
-        fill(v, 0, False)
-        fill(w, 2, False)
-
-    first = jnp.where(place == 0, 1, jnp.where(place == 1, 0, jnp.where(place == 2, 3, 2)))
-    second = jnp.where(place <= 1, 3, 0)
-    middle = jnp.where(place <= 1, 2, 1)
+    lower = place <= 1
 
     def system(block):
         return jnp.where(block == 3, last_ref[...], diags_ref[block]) + shift
 
-    inner = jnp.logical_or(place == 1, place == 2)
+    def choose(block, flipped, ref, turned_ref):
+        value = coups_ref[block]
+        turned = value.T
+        ref[...] = jnp.where(flipped, turned, value)
+        turned_ref[...] = jnp.where(flipped, value, turned)
+
+    first = jnp.where(place == 0, 1, jnp.where(place == 1, 0, jnp.where(place == 2, 3, 2)))
+    second = jnp.where(lower, 3, 0)
+    middle = jnp.where(lower, 2, 1)
+    choose(1, jnp.logical_not(lower), c_ref, ct_ref)
+    choose(jnp.where(lower, 2, 0), lower, v_ref, vt_ref)
+    choose(jnp.where(lower, 0, 2), lax.rem(place, 2) == 0, w_ref, wt_ref)
+
     invert([system(first), system(second)], [x_ref, y_ref])
     x = split(x_ref[...])
     y = split(y_ref[...])
-    w_s, wt_s = split(w_ref[...]), split(wt_ref[...])
-    xw = split(mul(x, w_s))
+    wt_s = split(wt_ref[...])
+    xw = split(mul(x, split(w_ref[...])))
     yv = split(mul(y, split(v_ref[...])))
-    rest = system(place) - mul(wt_s, xw)
-    reduced_ref[...] = rest
+    reduced_ref[...] = system(place) - mul(wt_s, xw)
     last_ref[...] = system(middle) - mul(split(vt_ref[...]), yv)
 
-    @pl.when(jnp.logical_not(inner))
+    @pl.when(jnp.logical_or(place == 0, place == 3))
     def _():
-        xu = split(mul(x, split(u_ref[...])))
-        ut_s = split(ut_ref[...])
+        xu = split(mul(x, split(c_ref[...])))
+        ut_s = split(ct_ref[...])
         last_ref[...] = last_ref[...] - mul(ut_s, xu)
         c_ref[...] = mul(wt_s, xu)
         ct_ref[...] = mul(ut_s, xw)
@@ -349,24 +343,24 @@
         for m in range(1, count - lag):
             total = total + samples[m] * samples[m + lag]
         scaled = bare * (total * scale)
-        result.append(bare / jnp.sqrt(1.0 + scaled * scaled))
+        result.append(bare * lax.rsqrt(1.0 + scaled * scaled))
     return result
 
 
-TAKEN_FIRST = 4
-TAKEN_SECOND = 13
+PAIRS_FIRST = 2
+PAIRS_SECOND = 7
 
 
 def regroup_kernel(
     count, base_ref, partial_ref, rows_ref, slots_ref, spread_ref, taken_ref,
-    lhs, arrived, bares, selfen, taken,
-    send_a, recv_a, send_b, recv_b, send_c, recv_c, send_d, recv_d,
+    lhs, outgoing, arrived, selfen, taken, send_a, recv_a, send_b, recv_b, send_c, recv_c,
 ):
     me = lax.axis_index("energy")
     width = base_ref.shape[0]
     half = width // 2
     chunk = rows_ref.shape[2]
     lines = taken.shape[1]
+    pairs = count // 2
 
     barrier = pltpu.get_barrier_semaphore()
 
@@ -376,6 +370,10 @@
         return carry
 
     lax.fori_loop(1, count, greet, 0)
+    for peer in range(count):
+        outgoing[peer, :8, :] = base_ref[peer * 8:peer * 8 + 8, :]
+        outgoing[peer, 8:, :] = partial_ref[peer * 8:peer * 8 + 8, :]
+    arrived[me] = outgoing[me]
 
     upper = base_ref[:half, :half]
     lower = base_ref[half:, half:]
@@ -384,60 +382,63 @@
     table = jnp.concatenate([jnp.where(r <= c, upper, lower), base_ref[:half, half:]], axis=1)
     diagonal = jnp.sum(jnp.where(r == c, lower, 0.0), axis=0, keepdims=True)
     extra = jnp.concatenate([jnp.zeros((1, half), F32), diagonal], axis=1)
-    first = lax.broadcasted_iota(jnp.int32, (16, width), 0) == 0
+    first = lax.broadcasted_iota(jnp.int32, (8, width), 0) == 0
     table = jnp.concatenate([table, jnp.where(first, extra, 0.0)], axis=0)
-    high, low = split(table)
     tall = table.shape[0]
-    used = half + 8
-    lhs[:tall, :] = high
-    lhs[tall:, :] = low
-    row_index = lax.broadcasted_iota(jnp.int32, (width, chunk), 0)
-    slot_index = lax.broadcasted_iota(jnp.int32, (used, chunk), 0)
+    high = table.astype(BF16).astype(F32)
+    lhs[...] = jnp.concatenate([high, table - high], axis=0).astype(BF16)
+    row_index = lax.broadcasted_iota(jnp.int32, (width, chunk), 0).astype(F32).astype(BF16)
+    line_index = lax.broadcasted_iota(jnp.int32, (8, chunk), 0)
+    one, none = jnp.bfloat16(1), jnp.bfloat16(0)
 
     def take(part):
-        hot = jnp.where(row_index == rows_ref[part], 1.0, 0.0).astype(BF16)
+        hot = jnp.where(row_index == rows_ref[part].astype(F32).astype(BF16), one, none)
         both = dot(lhs[...], hot)
-        found = jnp.where(slot_index == slots_ref[part], both[:used] + both[tall:tall + used], 0.0)
-        line = jnp.sum(found, axis=0, keepdims=True)
+        slots = slots_ref[part]
+        group = jnp.broadcast_to(lax.shift_right_logical(slots, 3), (8, chunk))
+        found, found_rest = both[:8], both[tall:tall + 8]
+        for at in range(1, tall // 8):
+            here = group == at
+            found = jnp.where(here, both[at * 8:at * 8 + 8], found)
+            found_rest = jnp.where(here, both[tall + at * 8:tall + at * 8 + 8], found_rest)
+        here = line_index == jnp.bitwise_and(slots, 7)
+        line = jnp.sum(jnp.where(here, found + found_rest, 0.0), axis=0, keepdims=True)
         for piece in range(chunk // 128):
             taken[part, piece:piece + 1, :] = line[:, piece * 128:(piece + 1) * 128]
         taken[part, chunk // 128:, :] = jnp.zeros((lines - chunk // 128, 128), F32)
 
-    source_a, target_a = lambda peer: rows_of(base_ref, peer), lambda slot: arrived.at[slot]
-    source_d, target_d = lambda peer: rows_of(partial_ref, peer), lambda slot: bares.at[slot]
+    source_a, target_a = lambda peer: outgoing.at[peer], lambda slot: arrived.at[slot]
     source_b, target_b = lambda peer: selfen.at[peer], lambda slot: rows_of(spread_ref, slot)
     source_c, target_c = lambda peer: taken.at[peer], lambda slot: taken_ref.at[slot]
 
-    def take_only(step, carry):
-        take(peer_of(me, count - step))
+    def take_pair(pair, carry):
+        take(peer_of(me, count - 1 - 2 * pair))
+        take(peer_of(me, count - 2 - 2 * pair))
         return carry
 
-    def send_only(step, carry):
-        block_copy(me, count - step, source_c, target_c, me, send_c, recv_c).start()
+    def send_pair(pair, carry):
+        for offset in (count - 1 - 2 * pair, count - 2 - 2 * pair):
+            block_copy(me, offset, source_c, target_c, me, send_c, recv_c).start()
         return carry
 
-    def take_and_send(step, carry):
-        take_only(step, carry)
-        return send_only(step, carry)
-
-    lax.fori_loop(1, 1 + TAKEN_FIRST, take_only, 0)
+    def take_and_send(pair, carry):
+        take_pair(pair, carry)
+        return send_pair(pair, carry)
+
+    lax.fori_loop(0, PAIRS_FIRST, take_pair, 0)
     pl.semaphore_wait(barrier, count - 1)
     send_blocks(count, me, source_a, target_a, send_a, recv_a)
-    send_blocks(count, me, source_d, target_d, send_d, recv_d)
-    lax.fori_loop(1, 1 + TAKEN_FIRST, send_only, 0)
-    arrived[me] = rows_of(base_ref, me)[...]
-    bares[me] = rows_of(partial_ref, me)[...]
-    lax.fori_loop(1 + TAKEN_FIRST, 1 + TAKEN_FIRST + TAKEN_SECOND, take_and_send, 0)
+    lax.fori_loop(0, PAIRS_FIRST, send_pair, 0)
+    lax.fori_loop(PAIRS_FIRST, PAIRS_FIRST + PAIRS_SECOND, take_and_send, 0)
     await_blocks(count, me, source_a, target_a, send_a, recv_a)
-    await_blocks(count, me, source_d, target_d, send_d, recv_d)
 
     scale = polar_coef * width / count
     for side in range(width // 128):
         cols = slice(side * 128, (side + 1) * 128)
-        bare = bares[0, :, cols]
+        bare = arrived[0, 8:, cols]
         for e in range(1, count):
-            bare = bare + bares[e, :, cols]
-        samples = [arrived[e, :, cols] for e in range(count)]
+            bare = bare + arrived[e, 8:, cols]
+        samples = [arrived[e, :8, cols] for e in range(count)]
         screened = screen(samples, bare, scale)
         for e in range(count):
             total = samples[e] * screened[0]
@@ -445,8 +446,9 @@
                 total = total + samples[e - n] * screened[n]
             selfen[e, :, cols] = total * (sigma_coef / count)
     send_blocks(count, me, source_b, target_b, send_b, recv_b)
-    lax.fori_loop(1 + TAKEN_FIRST + TAKEN_SECOND, count, take_and_send, 0)
-    take(me)
+    lax.fori_loop(PAIRS_FIRST + PAIRS_SECOND, pairs - 1, take_and_send, 0)
+    take_pair(pairs - 1, 0)
+    block_copy(me, 1, source_c, target_c, me, send_c, recv_c).start()
     taken_ref[me] = taken[me]
     spread_ref[pl.ds(pl.multiple_of(me * 8, 8), 8), :] = selfen[me]
     await_blocks(count, me, source_b, target_b, send_b, recv_b)
@@ -459,14 +461,7 @@
     chunk = screened_ref.shape[2]
     spread = spread_ref[...]
     matrix = reduced_ref[...] - 0.5 * (spread + spread.T)
-    base = base_ref[...]
-    residual = identity(width) - product(matrix, base)
-    x_ref[...] = base
-
-    @pl.when(jnp.logical_not(jnp.sum(residual * residual) < 0.5))
-    def _():
-        x_ref[...] = cold_start(matrix)
-
+    x_ref[...] = base_ref[...]
     settle([matrix], [x_ref])
     green_ref[0, 0] = x_ref[...]
     scale = polar_coef * width / count
@@ -506,7 +501,7 @@
             VMEM((count, 1, chunk), jnp.int32), VMEM((1, chunk), F32),
             DMA((2,)), DMA((2, 3)), DMA((2, 3)), DMA((2, 3)), DMA((2, 3)),
         ],
-        compiler_params=pltpu.CompilerParams(collective_id=0, has_side_effects=True),
+        compiler_params=pltpu.CompilerParams(collective_id=0, has_side_effects=True, vmem_limit_bytes=VMEM_LIMIT),
         name="collect",
     )(ham_diag, ham_coup, pattern, coulomb)
 
@@ -515,7 +510,8 @@
         out_shape=(square, square),
         in_specs=[smem, vmem, vmem],
         out_specs=(vmem, vmem),
-        scratch_shapes=[VMEM((width, width), F32)] * 11,
+        scratch_shapes=[VMEM((width, width), F32)] * 9,
+        compiler_params=pltpu.CompilerParams(vmem_limit_bytes=VMEM_LIMIT),
         name="chain",
     )(energies, diags, coups)
 
@@ -525,10 +521,10 @@
         in_specs=[vmem] * 4,
         out_specs=(vmem, vmem),
         scratch_shapes=[
-            VMEM((2 * (width // 2 + 16), width), BF16), VMEM((count, 8, width), F32),
-            VMEM((count, 8, width), F32), VMEM((count, 8, width), F32), VMEM((count, lines, 128), F32),
-        ] + [DMA((count,))] * 8,
-        compiler_params=pltpu.CompilerParams(collective_id=1, has_side_effects=True),
+            VMEM((width + 16, width), BF16), VMEM((count, 16, width), F32), VMEM((count, 16, width), F32),
+            VMEM((count, 8, width), F32), VMEM((count, lines, 128), F32),
+        ] + [DMA((count,))] * 6,
+        compiler_params=pltpu.CompilerParams(collective_id=1, has_side_effects=True, vmem_limit_bytes=VMEM_LIMIT),
         name="regroup",
     )(base, partial, rows, slots)
 
@@ -541,6 +537,7 @@
         in_specs=[vmem] * 5,
         out_specs=(vmem, vmem),
         scratch_shapes=[VMEM((width, width), F32)],
+        compiler_params=pltpu.CompilerParams(vmem_limit_bytes=VMEM_LIMIT),
         name="finish",
     )(reduced, base, spread, taken, bare_own)
 

time: 66.8 us -> 59.3 us (0.89)
  Pallas kernels: 65.3 us -> 54.2 us
  local copies, waits for them, and re-layouts: 0 us -> 3.5 us
    pallas_call x1, Pallas kernels: 14 us -> 10 us  [on_device(): pl.pallas_call(chain_kernel, out_shape=(square, square), in_specs=[smem,...]
    unnamed x0 -> x8, local copies, waits for them, and re-layouts: none -> 3.5 us
    pallas_call x1, Pallas kernels: 29.5 us -> 26.6 us  [on_device(): pl.pallas_call(functools.partial(regroup_kernel, count), out_shape=(squar...]
    pallas_call x1, Pallas kernels: 18 us -> 15.3 us  [on_device(): pl.pallas_call(functools.partial(collect_kernel, count, spaces), out_shap...]
    pallas_call x1, Pallas kernels: 3.8 us -> 2.26 us  [on_device(): pl.pallas_call(finish_kernel, out_shape=(jax.ShapeDtypeStruct((1, 1, widt...]
where the time goes in v3:
time: 59.3 us; the launch traced here: 59 us
  Pallas kernels  54.2 us (91%)
  local copies, waits for them, and re-layouts  3.5 us (6%)
  between operations  1.31 us (2%)
    pallas_call x1, Pallas kernels, on_device(): pl.pallas_call(functools.partial(regroup_kernel, count), out_shape=(squar...  26.6 us
    pallas_call x1, Pallas kernels, on_device(): pl.pallas_call(functools.partial(collect_kernel, count, spaces), out_shap...  15.3 us
    pallas_call x1, Pallas kernels, on_device(): pl.pallas_call(chain_kernel, out_shape=(square, square), in_specs=[smem,...  10 us
    unnamed x8, local copies, waits for them, and re-layouts  3.5 us
    pallas_call x1, Pallas kernels, on_device(): pl.pallas_call(finish_kernel, out_shape=(jax.ShapeDtypeStruct((1, 1, widt...  2.26 us

profile of v3, /device:TPU:1, one launch (start us, length us, event | category | flops | bytes accessed | tf_op | source)
XLA Modules:
  0.0 59.0 jit_solution(8385069413376941010)
XLA Ops:
  1.3 0.0 copy-start
  1.3 0.9 %copy-done = f32[1,256,256]{2,1,0:T(8,128)S(1)} copy-done((f32[1,256,256]{2,1,0:T(8,128)S(1)}, f32[1,256,256]{2,1,0:T(8,128)}, u32[]{:S(2)}) %copy-start) | copy-done | bytes 262168
  2.2 0.0 copy-start.1
  2.2 0.9 %copy-done.1 = f32[1,256,256]{2,1,0:T(8,128)S(1)} copy-done((f32[1,256,256]{2,1,0:T(8,128)S(1)}, f32[1,256,256]{2,1,0:T(8,128)}, u32[]{:S(2)}) %copy-start.1) | copy-done | bytes 262168
  3.2 0.0 copy-start.2
  3.2 0.9 %copy-done.2 = s32[1,43264]{1,0:T(1,128)S(1)} copy-done((s32[1,43264]{1,0:T(1,128)S(1)}, s32[1,43264]{1,0:T(1,128)}, u32[]{:S(2)}) %copy-start.2) | copy-done | bytes 173080
  4.1 0.0 copy-start.3
  4.1 0.7 %copy-done.3 = f32[1,1352]{1,0:T(1,128)S(1)} copy-done((f32[1,1352]{1,0:T(1,128)S(1)}, f32[1,1352]{1,0:T(1,128)}, u32[]{:S(2)}) %copy-start.3) | copy-done | bytes 5432
  4.8 15.3 %collect.1 = (f32[4,256,256]{2,1,0:T(8,128)S(1)}, f32[4,256,256]{2,1,0:T(8,128)S(1)}, s32[32,1,1408]{2,1,0:T(1,128)S(1)}, s32[32,1,1408]{2,1,0:T(1,128)S(1)}, f3...) custom-call(f32[1,256,256]{2,1,0:T(8,128)S(1)} %copy-done, f32[1,256,256]{2,1,0:T(8,128)S(1)} %copy-done.1, ...), custom_call_target="tpu_custom_call" | custom-call | tf_op jit(solution)/shard_map/collect/pallas_call | solution.py:488
  20.1 10.0 %chain.1 = (f32[256,256]{1,0:T(8,128)S(1)}, f32[256,256]{1,0:T(8,128)S(1)}) custom-call(f32[1]{0:T(128)S(6)} %copy.7.shift_ref, f32[4,256,256]{2,1,0:T(8,128)S(1)} %get-tuple-element.12.diags_ref, f32[4,256,256]{2,1,0:T(8,128)S(1)} %get-tuple-element.13.coups_ref), custom_call_target="tpu_custom_call" | custom-call | tf_op jit(solution)/shard_map/chain/pallas_call | solution.py:508
  30.1 26.6 %regroup.1 = (f32[256,256]{1,0:T(8,128)S(1)}, f32[32,16,128]{2,1,0:T(8,128)S(1)}) custom-call(f32[256,256]{1,0:T(8,128)S(1)} %get-tuple-element.15.base_ref, f32[256,256]{1,0:T(8,128)S(1)} %get-tuple-element.16.partial_ref, s32[32,1,1408]{2,1,0:T(1,128)S(1)} %get-tuple-element.17.rows_ref, s32[32,1,1408]{2,1,0:T(1,128)S(1)} %get-tuple-element.18.slots_ref), custom_call_target="tpu_custom_call" | custom-call | tf_op jit(solution)/shard_map/regroup/pallas_call | solution.py:518
  56.8 2.3 %finish.1 = (f32[1,1,256,256]{3,2,1,0:T(8,128)}, f32[32,1,1352]{2,1,0:T(1,128)}) custom-call(f32[256,256]{1,0:T(8,128)S(1)} %get-tuple-element.14.reduced_ref, f32[256,256]{1,0:T(8,128)S(1)} %get-tuple-element.15.base_ref, f32[256,256]{1,0:T(8,128)S(1)} %get-tuple-element.19.spread_ref, f32[32,16,128]{2,1,0:T(8,128)S(1)} %get-tuple-element.20.taken_ref, ...), custom_call_target="tpu_custom_call" | custom-call | tf_op jit(solution)/shard_map/finish/pallas_call | solution.py:531
Async XLA Ops:
  1.3 1.0 %copy-start = (f32[1,256,256]{2,1,0:T(8,128)S(1)}, f32[1,256,256]{2,1,0:T(8,128)}, u32[]{:S(2)}) copy-start(f32[1,256,256]{2,1,0:T(8,128)} %diag_ref.1) | copy-start | bytes 786436
  2.2 0.9 %copy-start.1 = (f32[1,256,256]{2,1,0:T(8,128)S(1)}, f32[1,256,256]{2,1,0:T(8,128)}, u32[]{:S(2)}) copy-start(f32[1,256,256]{2,1,0:T(8,128)} %coup_ref.1) | copy-start | bytes 786436
  3.2 0.9 %copy-start.2 = (s32[1,43264]{1,0:T(1,128)S(1)}, s32[1,43264]{1,0:T(1,128)}, u32[]{:S(2)}) copy-start(s32[1,43264]{1,0:T(1,128)} %pattern_ref.1) | copy-start | bytes 519172
  4.1 0.7 %copy-start.3 = (f32[1,1352]{1,0:T(1,128)S(1)}, f32[1,1352]{1,0:T(1,128)}, u32[]{:S(2)}) copy-start(f32[1,1352]{1,0:T(1,128)} %bare_ref.1) | copy-start | bytes 16228

commit v4 on v3

--- a/solution.py
+++ b/solution.py
@@ -171,8 +171,9 @@
 
 def collect_kernel(
     count, spaces, diag_ref, coup_ref, pattern_ref, bare_ref,
-    diags_ref, coups_ref, rows_ref, slots_ref, partial_ref, bare_own_ref,
-    own_pattern, own_bare, own_sem, far_send, far_recv, near_send, near_recv,
+    diags_ref, coups_ref, rows_ref, slots_ref, bare_pos_ref, bare_own_ref,
+    pattern, bare_in, own_pattern, own_bare, scattered, from_core, by_y, from_y, by_z, from_z,
+    own_sem, far_send, far_recv, near_send, near_recv, core_sems, y_send, y_recv, z_send, z_recv,
 ):
     me = lax.axis_index("energy")
     place = lax.axis_index("space")
@@ -180,16 +181,31 @@
     half = width // 2
     core = lax.rem(me, 2)
     other = me + 1 - 2 * core
+    own_y = lax.rem(me // 2, 4)
+    own_z = me // 8
     span = bare_ref.shape[1]
     chunk = own_bare.shape[1]
     sides = (lax.rem(place + 1, spaces), lax.rem(place + spaces - 1, spaces))
     across = lax.rem(place + 2, spaces)
 
+    own_copies = [
+        pltpu.make_async_copy(pattern_ref, pattern, own_sem.at[0]),
+        pltpu.make_async_copy(bare_ref, bare_in, own_sem.at[1]),
+        pltpu.make_async_copy(diag_ref.at[0], diags_ref.at[place], own_sem.at[2]),
+        pltpu.make_async_copy(coup_ref.at[0], coups_ref.at[place], own_sem.at[3]),
+    ]
+    for copy in own_copies:
+        copy.start()
+
     barrier = pltpu.get_barrier_semaphore()
     for side in sides:
         pl.semaphore_signal(barrier, inc=1, device_id={"space": side}, device_id_type=MESH)
+    for step in (2, 1, 3):
+        for stride in (2, 8):
+            pl.semaphore_signal(
+                barrier, inc=1, device_id={"energy": peer_of(me, step * stride)}, device_id_type=MESH)
     pl.semaphore_signal(barrier, inc=1, device_id={"energy": other}, device_id_type=MESH)
-    pl.semaphore_wait(barrier, 3)
+    pl.semaphore_wait(barrier, 9)
 
     own_half = pl.ds(pl.multiple_of(core * half, half), half)
     other_half = pl.ds(pl.multiple_of((1 - core) * half, half), half)
@@ -217,13 +233,9 @@
     for stage in range(2):
         for way in range(2):
             far(way, stage).start()
-    own_copies = [
-        pltpu.make_async_copy(diag_ref.at[0], diags_ref.at[place], own_sem.at[0]),
-        pltpu.make_async_copy(coup_ref.at[0], coups_ref.at[place], own_sem.at[1]),
-    ]
-    for copy in own_copies:
-        copy.start()
-
+
+    own_copies[0].wait()
+    own_copies[1].wait()
     tail = chunk - 128
     for part in range(count):
         size = chunk if part < count - 1 else span
@@ -231,7 +243,7 @@
             own_pattern[part, :, tail:] = jnp.zeros((1, 128), jnp.int32)
             rows_ref[part, :, tail:] = jnp.zeros((1, 128), jnp.int32)
             slots_ref[part, :, tail:] = jnp.zeros((1, 128), jnp.int32)
-        piece = pattern_ref[:, part * span:part * span + size]
+        piece = pattern[:, part * span:part * span + size]
         own_pattern[part, :, :size] = piece
         row = lax.shift_right_logical(piece, 8)
         col = jnp.bitwise_and(piece, 255)
@@ -242,12 +254,7 @@
         rows_ref[part, :, :size] = jnp.where(jnp.logical_and(lower, jnp.logical_not(pivot)), low - 128, high)
         slots_ref[part, :, :size] = jnp.where(lower, jnp.where(pivot, 128, high - 128), low)
     own_bare[:, tail:] = jnp.zeros((1, 128), F32)
-    own_bare[:, :span] = bare_ref[...]
-
-    for way in range(2):
-        far(way, 0).wait_recv()
-        far(way, 2).start()
-        near(way, 0, own_half).start()
+    own_bare[:, :span] = bare_in[...]
 
     mine = own_pattern[me]
     bare = own_bare[...]
@@ -261,17 +268,58 @@
         rest = rest - part
         term = dot_nt(jnp.where(on_row, part, 0.0).astype(BF16), on_col)
         total = term if total is None else total + term
-    partial_ref[...] = total
+    for peer in range(count):
+        scattered[peer % 2, peer // 2 % 4, peer // 8] = total[peer * 8:peer * 8 + 8, :]
     for line in range(chunk // 128):
         bare_own_ref[line:line + 1, :] = bare[:, line * 128:(line + 1) * 128]
     for line in range(chunk // 128, bare_own_ref.shape[0]):
         bare_own_ref[line:line + 1, :] = jnp.zeros((1, 128), F32)
 
-    for stage in (1, 2):
-        for way in range(2):
-            far(way, stage).wait_recv()
-            near(way, stage, own_half).start()
-    for copy in own_copies:
+    for way in range(2):
+        far(way, 0).wait_recv()
+        far(way, 2).start()
+        near(way, 0, own_half).start()
+
+    to_core = pltpu.make_async_remote_copy(
+        src_ref=scattered.at[1 - core], dst_ref=from_core,
+        send_sem=core_sems.at[0], recv_sem=core_sems.at[1],
+        device_id={"energy": other}, device_id_type=MESH)
+
+    def to_y(step):
+        return pltpu.make_async_remote_copy(
+            src_ref=by_y.at[lax.rem(own_y + step, 4)], dst_ref=from_y.at[step],
+            send_sem=y_send.at[step], recv_sem=y_recv.at[step],
+            device_id={"energy": peer_of(me, 2 * step)}, device_id_type=MESH)
+
+    def to_z(step):
+        return pltpu.make_async_remote_copy(
+            src_ref=by_z.at[lax.rem(own_z + step, 4)], dst_ref=from_z.at[step],
+            send_sem=z_send.at[step], recv_sem=z_recv.at[step],
+            device_id={"energy": peer_of(me, 8 * step)}, device_id_type=MESH)
+
+    to_core.start()
+    to_core.wait()
+    for y in range(4):
+        for z in range(4):
+            by_y[y, z] = scattered[core, y, z] + from_core[y, z]
+    for step in (2, 1, 3):
+        to_y(step).start()
+    for way in range(2):
+        far(way, 1).wait_recv()
+        near(way, 1, own_half).start()
+    for step in (1, 3, 2):
+        to_y(step).wait()
+    for z in range(4):
+        by_z[z] = (by_y[own_y, z] + from_y[1, z]) + (from_y[2, z] + from_y[3, z])
+    for step in (2, 1, 3):
+        to_z(step).start()
+    for way in range(2):
+        far(way, 2).wait_recv()
+        near(way, 2, own_half).start()
+    for step in (1, 3, 2):
+        to_z(step).wait()
+    bare_pos_ref[...] = (by_z[own_z] + from_z[1]) + (from_z[2] + from_z[3])
+    for copy in own_copies[2:]:
         copy.wait()
     for stage in range(3):
         for way in range(2):
@@ -352,8 +400,8 @@
 
 
 def regroup_kernel(
-    count, base_ref, partial_ref, rows_ref, slots_ref, spread_ref, taken_ref,
-    lhs, outgoing, arrived, selfen, taken, send_a, recv_a, send_b, recv_b, send_c, recv_c,
+    count, base_ref, rows_ref, slots_ref, bare_pos_ref, spread_ref, taken_ref,
+    lhs, arrived, selfen, taken, send_a, recv_a, send_b, recv_b, send_c, recv_c,
 ):
     me = lax.axis_index("energy")
     width = base_ref.shape[0]
@@ -370,10 +418,7 @@
         return carry
 
     lax.fori_loop(1, count, greet, 0)
-    for peer in range(count):
-        outgoing[peer, :8, :] = base_ref[peer * 8:peer * 8 + 8, :]
-        outgoing[peer, 8:, :] = partial_ref[peer * 8:peer * 8 + 8, :]
-    arrived[me] = outgoing[me]
+    arrived[me] = rows_of(base_ref, me)[...]
 
     upper = base_ref[:half, :half]
     lower = base_ref[half:, half:]
@@ -407,7 +452,7 @@
             taken[part, piece:piece + 1, :] = line[:, piece * 128:(piece + 1) * 128]
         taken[part, chunk // 128:, :] = jnp.zeros((lines - chunk // 128, 128), F32)
 
-    source_a, target_a = lambda peer: outgoing.at[peer], lambda slot: arrived.at[slot]
+    source_a, target_a = lambda peer: rows_of(base_ref, peer), lambda slot: arrived.at[slot]
     source_b, target_b = lambda peer: selfen.at[peer], lambda slot: rows_of(spread_ref, slot)
     source_c, target_c = lambda peer: taken.at[peer], lambda slot: taken_ref.at[slot]
 
@@ -435,11 +480,8 @@
     scale = polar_coef * width / count
     for side in range(width // 128):
         cols = slice(side * 128, (side + 1) * 128)
-        bare = arrived[0, 8:, cols]
-        for e in range(1, count):
-            bare = bare + arrived[e, 8:, cols]
-        samples = [arrived[e, :8, cols] for e in range(count)]
-        screened = screen(samples, bare, scale)
+        samples = [arrived[e, :, cols] for e in range(count)]
+        screened = screen(samples, bare_pos_ref[:, cols], scale)
         for e in range(count):
             total = samples[e] * screened[0]
             for n in range(1, e + 1):
@@ -485,25 +527,29 @@
     vmem = pl.BlockSpec(memory_space=pltpu.VMEM)
     smem = pl.BlockSpec(memory_space=pltpu.SMEM)
     square = jax.ShapeDtypeStruct((width, width), F32)
-    diags, coups, rows, slots, partial, bare_own = pl.pallas_call(
+    diags, coups, rows, slots, bare_pos, bare_own = pl.pallas_call(
         functools.partial(collect_kernel, count, spaces),
         out_shape=(
             jax.ShapeDtypeStruct((spaces, width, width), F32),
             jax.ShapeDtypeStruct((spaces, width, width), F32),
             jax.ShapeDtypeStruct((count, 1, chunk), jnp.int32),
             jax.ShapeDtypeStruct((count, 1, chunk), jnp.int32),
-            square,
+            jax.ShapeDtypeStruct((8, width), F32),
             jax.ShapeDtypeStruct((lines, 128), F32),
         ),
-        in_specs=[vmem] * 4,
+        in_specs=[pl.BlockSpec(memory_space=pltpu.HBM)] * 4,
         out_specs=(vmem,) * 6,
         scratch_shapes=[
+            VMEM((1, pattern.shape[1]), jnp.int32), VMEM((1, span), F32),
             VMEM((count, 1, chunk), jnp.int32), VMEM((1, chunk), F32),
-            DMA((2,)), DMA((2, 3)), DMA((2, 3)), DMA((2, 3)), DMA((2, 3)),
+            VMEM((2, 4, 4, 8, width), F32), VMEM((4, 4, 8, width), F32), VMEM((4, 4, 8, width), F32),
+            VMEM((4, 4, 8, width), F32), VMEM((4, 8, width), F32), VMEM((4, 8, width), F32),
+            DMA((4,)), DMA((2, 3)), DMA((2, 3)), DMA((2, 3)), DMA((2, 3)),
+            DMA((2,)), DMA((4,)), DMA((4,)), DMA((4,)), DMA((4,)),
         ],
         compiler_params=pltpu.CompilerParams(collective_id=0, has_side_effects=True, vmem_limit_bytes=VMEM_LIMIT),
         name="collect",
-    )(ham_diag, ham_coup, pattern, coulomb)
+    )(*(pltpu.with_memory_space_constraint(value, pltpu.HBM) for value in (ham_diag, ham_coup, pattern, coulomb)))
 
     reduced, base = pl.pallas_call(
         chain_kernel,
@@ -521,12 +567,12 @@
         in_specs=[vmem] * 4,
         out_specs=(vmem, vmem),
         scratch_shapes=[
-            VMEM((width + 16, width), BF16), VMEM((count, 16, width), F32), VMEM((count, 16, width), F32),
+            VMEM((width + 16, width), BF16), VMEM((count, 8, width), F32),
             VMEM((count, 8, width), F32), VMEM((count, lines, 128), F32),
         ] + [DMA((count,))] * 6,
         compiler_params=pltpu.CompilerParams(collective_id=1, has_side_effects=True, vmem_limit_bytes=VMEM_LIMIT),
         name="regroup",
-    )(base, partial, rows, slots)
+    )(base, rows, slots, bare_pos)
 
     return pl.pallas_call(
         finish_kernel,

time: 59.3 us -> 57.8 us (0.975)
  local copies, waits for them, and re-layouts: 3.5 us -> 0 us
  Pallas kernels: 54.2 us -> 56.4 us
    pallas_call x1, Pallas kernels: 15.3 us -> 22 us  [on_device(): pl.pallas_call(functools.partial(collect_kernel, count, spaces), out_shap...]
    pallas_call x1, Pallas kernels: 26.6 us -> 22.1 us  [on_device(): pl.pallas_call(functools.partial(regroup_kernel, count), out_shape=(squar...]
    unnamed x8 -> x0, local copies, waits for them, and re-layouts: 3.5 us -> none
where the time goes in v4:
time: 57.8 us; the launch traced here: 57.7 us
  Pallas kernels  56.4 us (98%)
  between operations  1.3 us (2%)
    pallas_call x1, Pallas kernels, on_device(): pl.pallas_call(functools.partial(regroup_kernel, count), out_shape=(squar...  22.1 us
    pallas_call x1, Pallas kernels, on_device(): pl.pallas_call(functools.partial(collect_kernel, count, spaces), out_shap...  22 us
    pallas_call x1, Pallas kernels, on_device(): pl.pallas_call(chain_kernel, out_shape=(square, square), in_specs=[smem,...  10 us
    pallas_call x1, Pallas kernels, on_device(): pl.pallas_call(finish_kernel, out_shape=(jax.ShapeDtypeStruct((1, 1, widt...  2.26 us

profile of v4, /device:TPU:1, one launch (start us, length us, event | category | flops | bytes accessed | tf_op | source)
XLA Modules:
  0.0 57.7 jit_solution(10552977467620915646)
XLA Ops:
  1.3 22.0 %collect.1 = (f32[4,256,256]{2,1,0:T(8,128)S(1)}, f32[4,256,256]{2,1,0:T(8,128)S(1)}, s32[32,1,1408]{2,1,0:T(1,128)S(1)}, s32[32,1,1408]{2,1,0:T(1,128)S(1)}, f3...) custom-call(f32[1,256,256]{2,1,0:T(8,128)} %diag_ref.1, f32[1,256,256]{2,1,0:T(8,128)} %coup_ref.1, s32[1,43264]{1,0:T(1,128)} %pattern_ref.1, ...), custom_call_target="tpu_custom_call" | custom-call | tf_op jit(solution)/shard_map/collect/pallas_call | solution.py:530
  23.3 10.0 %chain.1 = (f32[256,256]{1,0:T(8,128)S(1)}, f32[256,256]{1,0:T(8,128)S(1)}) custom-call(f32[1]{0:T(128)S(6)} %copy.7.shift_ref, f32[4,256,256]{2,1,0:T(8,128)S(1)} %get-tuple-element.12.diags_ref, f32[4,256,256]{2,1,0:T(8,128)S(1)} %get-tuple-element.13.coups_ref), custom_call_target="tpu_custom_call" | custom-call | tf_op jit(solution)/shard_map/chain/pallas_call | solution.py:554
  33.3 22.1 %regroup.1 = (f32[256,256]{1,0:T(8,128)S(1)}, f32[32,16,128]{2,1,0:T(8,128)S(1)}) custom-call(f32[256,256]{1,0:T(8,128)S(1)} %get-tuple-element.15.base_ref, s32[32,1,1408]{2,1,0:T(1,128)S(1)} %get-tuple-element.16.rows_ref, s32[32,1,1408]{2,1,0:T(1,128)S(1)} %get-tuple-element.17.slots_ref, f32[8,256]{1,0:T(8,128)S(1)} %get-tuple-element.18.bare_pos_ref), custom_call_target="tpu_custom_call" | custom-call | tf_op jit(solution)/shard_map/regroup/pallas_call | solution.py:564
  55.4 2.3 %finish.1 = (f32[1,1,256,256]{3,2,1,0:T(8,128)}, f32[32,1,1352]{2,1,0:T(1,128)}) custom-call(f32[256,256]{1,0:T(8,128)S(1)} %get-tuple-element.14.reduced_ref, f32[256,256]{1,0:T(8,128)S(1)} %get-tuple-element.15.base_ref, f32[256,256]{1,0:T(8,128)S(1)} %get-tuple-element.19.spread_ref, f32[32,16,128]{2,1,0:T(8,128)S(1)} %get-tuple-element.20.taken_ref, ...), custom_call_target="tpu_custom_call" | custom-call | tf_op jit(solution)/shard_map/finish/pallas_call | solution.py:577

commit v5 on v4

--- a/solution.py
+++ b/solution.py
@@ -15,7 +15,7 @@
 polar_coef = 128.0
 sigma_coef = 0.5
 
-TOLERANCE = 1e-6
+TOLERANCE = 1e-5
 VMEM_LIMIT = 20 << 20
 
 
@@ -49,7 +49,10 @@
 def series(matrix, alpha, doublings):
     power = identity(matrix.shape[0]) - matrix * alpha
     guess = alpha * (identity(matrix.shape[0]) + power)
-    for _ in range(doublings):
+    parts = split(power)
+    power = mul(parts, parts)
+    guess = guess + product(guess, power)
+    for _ in range(doublings - 1):
         high = power.astype(BF16)
         power = dot(high, high)
         guess = guess + dot(guess.astype(BF16), power.astype(BF16))
@@ -205,34 +208,6 @@
             pl.semaphore_signal(
                 barrier, inc=1, device_id={"energy": peer_of(me, step * stride)}, device_id_type=MESH)
     pl.semaphore_signal(barrier, inc=1, device_id={"energy": other}, device_id_type=MESH)
-    pl.semaphore_wait(barrier, 9)
-
-    own_half = pl.ds(pl.multiple_of(core * half, half), half)
-    other_half = pl.ds(pl.multiple_of((1 - core) * half, half), half)
-    given = (diag_ref, coup_ref)
-    stores = (diags_ref, coups_ref)
-
-    def far(way, stage):
-        kind = (way, 1 - way, way)[stage]
-        block = place if stage < 2 else sides[1 - way]
-        source = given[kind].at[0, own_half] if stage < 2 else stores[kind].at[block, own_half]
-        return pltpu.make_async_remote_copy(
-            src_ref=source, dst_ref=stores[kind].at[block, own_half],
-            send_sem=far_send.at[way, stage], recv_sem=far_recv.at[way, stage],
-            device_id={"space": sides[way]}, device_id_type=MESH)
-
-    def near(way, stage, part):
-        kind = (way, 1 - way, way)[stage]
-        block = sides[1 - way] if stage < 2 else across
-        piece = stores[kind].at[block, part]
-        return pltpu.make_async_remote_copy(
-            src_ref=piece, dst_ref=piece,
-            send_sem=near_send.at[way, stage], recv_sem=near_recv.at[way, stage],
-            device_id={"energy": other}, device_id_type=MESH)
-
-    for stage in range(2):
-        for way in range(2):
-            far(way, stage).start()
 
     own_copies[0].wait()
     own_copies[1].wait()
@@ -256,6 +231,34 @@
     own_bare[:, tail:] = jnp.zeros((1, 128), F32)
     own_bare[:, :span] = bare_in[...]
 
+    pl.semaphore_wait(barrier, 9)
+    own_half = pl.ds(pl.multiple_of(core * half, half), half)
+    other_half = pl.ds(pl.multiple_of((1 - core) * half, half), half)
+    given = (diag_ref, coup_ref)
+    stores = (diags_ref, coups_ref)
+
+    def far(way, stage):
+        kind = (way, 1 - way, way)[stage]
+        block = place if stage < 2 else sides[1 - way]
+        source = given[kind].at[0, own_half] if stage < 2 else stores[kind].at[block, own_half]
+        return pltpu.make_async_remote_copy(
+            src_ref=source, dst_ref=stores[kind].at[block, own_half],
+            send_sem=far_send.at[way, stage], recv_sem=far_recv.at[way, stage],
+            device_id={"space": sides[way]}, device_id_type=MESH)
+
+    def near(way, stage, part):
+        kind = (way, 1 - way, way)[stage]
+        block = sides[1 - way] if stage < 2 else across
+        piece = stores[kind].at[block, part]
+        return pltpu.make_async_remote_copy(
+            src_ref=piece, dst_ref=piece,
+            send_sem=near_send.at[way, stage], recv_sem=near_recv.at[way, stage],
+            device_id={"energy": other}, device_id_type=MESH)
+
+    for stage in range(2):
+        for way in range(2):
+            far(way, stage).start()
+
     mine = own_pattern[me]
     bare = own_bare[...]
     index = lax.broadcasted_iota(jnp.int32, (width, chunk), 0)
@@ -275,11 +278,6 @@
     for line in range(chunk // 128, bare_own_ref.shape[0]):
         bare_own_ref[line:line + 1, :] = jnp.zeros((1, 128), F32)
 
-    for way in range(2):
-        far(way, 0).wait_recv()
-        far(way, 2).start()
-        near(way, 0, own_half).start()
-
     to_core = pltpu.make_async_remote_copy(
         src_ref=scattered.at[1 - core], dst_ref=from_core,
         send_sem=core_sems.at[0], recv_sem=core_sems.at[1],
@@ -298,24 +296,26 @@
             device_id={"energy": peer_of(me, 8 * step)}, device_id_type=MESH)
 
     to_core.start()
+    for way in range(2):
+        far(way, 0).wait_recv()
+        far(way, 2).start()
+        near(way, 0, own_half).start()
     to_core.wait()
     for y in range(4):
         for z in range(4):
             by_y[y, z] = scattered[core, y, z] + from_core[y, z]
     for step in (2, 1, 3):
         to_y(step).start()
-    for way in range(2):
-        far(way, 1).wait_recv()
-        near(way, 1, own_half).start()
     for step in (1, 3, 2):
         to_y(step).wait()
     for z in range(4):
         by_z[z] = (by_y[own_y, z] + from_y[1, z]) + (from_y[2, z] + from_y[3, z])
     for step in (2, 1, 3):
         to_z(step).start()
-    for way in range(2):
-        far(way, 2).wait_recv()
-        near(way, 2, own_half).start()
+    for stage in (1, 2):
+        for way in range(2):
+            far(way, stage).wait_recv()
+            near(way, stage, own_half).start()
     for step in (1, 3, 2):
         to_z(step).wait()
     bare_pos_ref[...] = (by_z[own_z] + from_z[1]) + (from_z[2] + from_z[3])
@@ -396,7 +396,7 @@
 
 
 PAIRS_FIRST = 2
-PAIRS_SECOND = 7
+PAIRS_SECOND = 9
 
 
 def regroup_kernel(
@@ -409,6 +409,8 @@
     chunk = rows_ref.shape[2]
     lines = taken.shape[1]
     pairs = count // 2
+    for peer in range(count):
+        taken_ref[peer, chunk // 128:, :] = jnp.zeros((lines - chunk // 128, 128), F32)
 
     barrier = pltpu.get_barrier_semaphore()
 
@@ -450,11 +452,11 @@
         line = jnp.sum(jnp.where(here, found + found_rest, 0.0), axis=0, keepdims=True)
         for piece in range(chunk // 128):
             taken[part, piece:piece + 1, :] = line[:, piece * 128:(piece + 1) * 128]
-        taken[part, chunk // 128:, :] = jnp.zeros((lines - chunk // 128, 128), F32)
 
     source_a, target_a = lambda peer: rows_of(base_ref, peer), lambda slot: arrived.at[slot]
     source_b, target_b = lambda peer: selfen.at[peer], lambda slot: rows_of(spread_ref, slot)
-    source_c, target_c = lambda peer: taken.at[peer], lambda slot: taken_ref.at[slot]
+    filled = chunk // 128
+    source_c, target_c = lambda peer: taken.at[peer, :filled], lambda slot: taken_ref.at[slot, :filled]
 
     def take_pair(pair, carry):
         take(peer_of(me, count - 1 - 2 * pair))
@@ -491,7 +493,7 @@
     lax.fori_loop(PAIRS_FIRST + PAIRS_SECOND, pairs - 1, take_and_send, 0)
     take_pair(pairs - 1, 0)
     block_copy(me, 1, source_c, target_c, me, send_c, recv_c).start()
-    taken_ref[me] = taken[me]
+    taken_ref[me, :filled] = taken[me, :filled]
     spread_ref[pl.ds(pl.multiple_of(me * 8, 8), 8), :] = selfen[me]
     await_blocks(count, me, source_b, target_b, send_b, recv_b)
     await_blocks(count, me, source_c, target_c, send_c, recv_c)

time: 57.8 us -> 54 us (0.934)
  Pallas kernels: 56.4 us -> 52.5 us
    pallas_call x1, Pallas kernels: 22 us -> 20.1 us  [on_device(): pl.pallas_call(functools.partial(collect_kernel, count, spaces), out_shap...]
    pallas_call x1, Pallas kernels: 10 us -> 8.73 us  [on_device(): pl.pallas_call(chain_kernel, out_shape=(square, square), in_specs=[smem,...]
    pallas_call x1, Pallas kernels: 22.1 us -> 21.4 us  [on_device(): pl.pallas_call(functools.partial(regroup_kernel, count), out_shape=(squar...]
where the time goes in v5:
time: 54 us; the launch traced here: 53.8 us
  Pallas kernels  52.5 us (97%)
  between operations  1.3 us (2%)
    pallas_call x1, Pallas kernels, on_device(): pl.pallas_call(functools.partial(regroup_kernel, count), out_shape=(squar...  21.4 us
    pallas_call x1, Pallas kernels, on_device(): pl.pallas_call(functools.partial(collect_kernel, count, spaces), out_shap...  20.1 us
    pallas_call x1, Pallas kernels, on_device(): pl.pallas_call(chain_kernel, out_shape=(square, square), in_specs=[smem,...  8.73 us
    pallas_call x1, Pallas kernels, on_device(): pl.pallas_call(finish_kernel, out_shape=(jax.ShapeDtypeStruct((1, 1, widt...  2.27 us

profile of v5, /device:TPU:1, one launch (start us, length us, event | category | flops | bytes accessed | tf_op | source)
XLA Modules:
  0.0 53.8 jit_solution(9777908383843077544)
XLA Ops:
  1.3 20.1 %collect.1 = (f32[4,256,256]{2,1,0:T(8,128)S(1)}, f32[4,256,256]{2,1,0:T(8,128)S(1)}, s32[32,1,1408]{2,1,0:T(1,128)S(1)}, s32[32,1,1408]{2,1,0:T(1,128)S(1)}, f3...) custom-call(f32[1,256,256]{2,1,0:T(8,128)} %diag_ref.1, f32[1,256,256]{2,1,0:T(8,128)} %coup_ref.1, s32[1,43264]{1,0:T(1,128)} %pattern_ref.1, ...), custom_call_target="tpu_custom_call" | custom-call | tf_op jit(solution)/shard_map/collect/pallas_call | solution.py:532
  21.4 8.7 %chain.1 = (f32[256,256]{1,0:T(8,128)S(1)}, f32[256,256]{1,0:T(8,128)S(1)}) custom-call(f32[1]{0:T(128)S(6)} %copy.7.shift_ref, f32[4,256,256]{2,1,0:T(8,128)S(1)} %get-tuple-element.12.diags_ref, f32[4,256,256]{2,1,0:T(8,128)S(1)} %get-tuple-element.13.coups_ref), custom_call_target="tpu_custom_call" | custom-call | tf_op jit(solution)/shard_map/chain/pallas_call | solution.py:556
  30.2 21.4 %regroup.1 = (f32[256,256]{1,0:T(8,128)S(1)}, f32[32,16,128]{2,1,0:T(8,128)S(1)}) custom-call(f32[256,256]{1,0:T(8,128)S(1)} %get-tuple-element.15.base_ref, s32[32,1,1408]{2,1,0:T(1,128)S(1)} %get-tuple-element.16.rows_ref, s32[32,1,1408]{2,1,0:T(1,128)S(1)} %get-tuple-element.17.slots_ref, f32[8,256]{1,0:T(8,128)S(1)} %get-tuple-element.18.bare_pos_ref), custom_call_target="tpu_custom_call" | custom-call | tf_op jit(solution)/shard_map/regroup/pallas_call | solution.py:566
  51.6 2.3 %finish.1 = (f32[1,1,256,256]{3,2,1,0:T(8,128)}, f32[32,1,1352]{2,1,0:T(1,128)}) custom-call(f32[256,256]{1,0:T(8,128)S(1)} %get-tuple-element.14.reduced_ref, f32[256,256]{1,0:T(8,128)S(1)} %get-tuple-element.15.base_ref, f32[256,256]{1,0:T(8,128)S(1)} %get-tuple-element.19.spread_ref, f32[32,16,128]{2,1,0:T(8,128)S(1)} %get-tuple-element.20.taken_ref, ...), custom_call_target="tpu_custom_call" | custom-call | tf_op jit(solution)/shard_map/finish/pallas_call | solution.py:579

commit v6 on v5

--- a/solution.py
+++ b/solution.py
@@ -47,10 +47,10 @@
 
 
 def series(matrix, alpha, doublings):
-    power = identity(matrix.shape[0]) - matrix * alpha
-    guess = alpha * (identity(matrix.shape[0]) + power)
-    parts = split(power)
-    power = mul(parts, parts)
+    ident = identity(matrix.shape[0])
+    parts = split(matrix)
+    power = ident - matrix * (2.0 * alpha) + mul(parts, parts) * (alpha * alpha)
+    guess = alpha * (2.0 * ident - matrix * alpha)
     guess = guess + product(guess, power)
     for _ in range(doublings - 1):
         high = power.astype(BF16)
@@ -140,32 +140,18 @@
     return z * 8 + y * 2 + core
 
 
-def block_copy(me, offset, source, target, slot, send_sems, recv_sems):
-    peer = peer_of(me, offset)
+def peers_of(count, me):
+    cores = [lax.rem(me + step, 2) for step in range(2)]
+    ys = [lax.rem(me // 2 + step, 4) * 2 for step in range(4)]
+    zs = [lax.rem(me // 8 + step, 4) * 8 for step in range(4)]
+    return [zs[offset // 8] + ys[offset // 2 % 4] + cores[offset % 2] for offset in range(count - 1, 0, -1)]
+
+
+def to_peer(peer, source, target, sems):
     return pltpu.make_async_remote_copy(
-        src_ref=source(peer), dst_ref=target(slot),
-        send_sem=send_sems.at[offset], recv_sem=recv_sems.at[slot],
+        src_ref=source, dst_ref=target, send_sem=sems.at[0], recv_sem=sems.at[1],
         device_id={"energy": peer}, device_id_type=MESH,
     )
-
-
-def send_blocks(count, me, source, target, send_sems, recv_sems):
-    def one(step, carry):
-        block_copy(me, count - step, source, target, me, send_sems, recv_sems).start()
-        return carry
-
-    lax.fori_loop(1, count, one, 0)
-
-
-def await_blocks(count, me, source, target, send_sems, recv_sems):
-    def one(step, carry):
-        offset = count - step
-        copy = block_copy(me, offset, source, target, peer_of(me, offset), send_sems, recv_sems)
-        copy.wait_send()
-        copy.wait_recv()
-        return carry
-
-    lax.fori_loop(1, count, one, 0)
 
 
 def rows_of(ref, peer):
@@ -401,7 +387,7 @@
 
 def regroup_kernel(
     count, base_ref, rows_ref, slots_ref, bare_pos_ref, spread_ref, taken_ref,
-    lhs, arrived, selfen, taken, send_a, recv_a, send_b, recv_b, send_c, recv_c,
+    lhs, arrived, selfen, taken, sems_a, sems_b, sems_c,
 ):
     me = lax.axis_index("energy")
     width = base_ref.shape[0]
@@ -414,12 +400,9 @@
 
     barrier = pltpu.get_barrier_semaphore()
 
-    def greet(step, carry):
-        pl.semaphore_signal(
-            barrier, inc=1, device_id={"energy": peer_of(me, count - step)}, device_id_type=MESH)
-        return carry
-
-    lax.fori_loop(1, count, greet, 0)
+    others = peers_of(count, me)
+    for peer in others:
+        pl.semaphore_signal(barrier, inc=1, device_id={"energy": peer}, device_id_type=MESH)
     arrived[me] = rows_of(base_ref, me)[...]
 
     upper = base_ref[:half, :half]
@@ -453,19 +436,22 @@
         for piece in range(chunk // 128):
             taken[part, piece:piece + 1, :] = line[:, piece * 128:(piece + 1) * 128]
 
-    source_a, target_a = lambda peer: rows_of(base_ref, peer), lambda slot: arrived.at[slot]
-    source_b, target_b = lambda peer: selfen.at[peer], lambda slot: rows_of(spread_ref, slot)
     filled = chunk // 128
-    source_c, target_c = lambda peer: taken.at[peer, :filled], lambda slot: taken_ref.at[slot, :filled]
+
+    def all_but_one(source, target, sems):
+        return to_peer(others[0], source, target, sems)
 
     def take_pair(pair, carry):
         take(peer_of(me, count - 1 - 2 * pair))
         take(peer_of(me, count - 2 - 2 * pair))
         return carry
 
+    def send_taken(peer):
+        to_peer(peer, taken.at[peer, :filled], taken_ref.at[me, :filled], sems_c).start()
+
     def send_pair(pair, carry):
         for offset in (count - 1 - 2 * pair, count - 2 - 2 * pair):
-            block_copy(me, offset, source_c, target_c, me, send_c, recv_c).start()
+            send_taken(peer_of(me, offset))
         return carry
 
     def take_and_send(pair, carry):
@@ -474,10 +460,14 @@
 
     lax.fori_loop(0, PAIRS_FIRST, take_pair, 0)
     pl.semaphore_wait(barrier, count - 1)
-    send_blocks(count, me, source_a, target_a, send_a, recv_a)
+    for peer in others:
+        to_peer(peer, rows_of(base_ref, peer), arrived.at[me], sems_a).start()
     lax.fori_loop(0, PAIRS_FIRST, send_pair, 0)
     lax.fori_loop(PAIRS_FIRST, PAIRS_FIRST + PAIRS_SECOND, take_and_send, 0)
-    await_blocks(count, me, source_a, target_a, send_a, recv_a)
+    rest = pl.ds(8, width - 8)
+    first_exchange = all_but_one(base_ref.at[rest, :], arrived.at[pl.ds(1, count - 1)], sems_a)
+    first_exchange.wait_send()
+    first_exchange.wait_recv()
 
     scale = polar_coef * width / count
     for side in range(width // 128):
@@ -489,14 +479,19 @@
             for n in range(1, e + 1):
                 total = total + samples[e - n] * screened[n]
             selfen[e, :, cols] = total * (sigma_coef / count)
-    send_blocks(count, me, source_b, target_b, send_b, recv_b)
+    for peer in others:
+        to_peer(peer, selfen.at[peer], rows_of(spread_ref, me), sems_b).start()
     lax.fori_loop(PAIRS_FIRST + PAIRS_SECOND, pairs - 1, take_and_send, 0)
     take_pair(pairs - 1, 0)
-    block_copy(me, 1, source_c, target_c, me, send_c, recv_c).start()
+    send_taken(peer_of(me, 1))
     taken_ref[me, :filled] = taken[me, :filled]
     spread_ref[pl.ds(pl.multiple_of(me * 8, 8), 8), :] = selfen[me]
-    await_blocks(count, me, source_b, target_b, send_b, recv_b)
-    await_blocks(count, me, source_c, target_c, send_c, recv_c)
+    for last_exchange in (
+        all_but_one(selfen.at[pl.ds(1, count - 1)], spread_ref.at[rest, :], sems_b),
+        all_but_one(taken.at[pl.ds(1, count - 1), :filled], taken_ref.at[pl.ds(1, count - 1), :filled], sems_c),
+    ):
+        last_exchange.wait_send()
+        last_exchange.wait_recv()
 
 
 def finish_kernel(reduced_ref, base_ref, spread_ref, taken_ref, bare_ref, green_ref, screened_ref, x_ref):
@@ -571,7 +566,7 @@
         scratch_shapes=[
             VMEM((width + 16, width), BF16), VMEM((count, 8, width), F32),
             VMEM((count, 8, width), F32), VMEM((count, lines, 128), F32),
-        ] + [DMA((count,))] * 6,
+        ] + [DMA((2,))] * 3,
         compiler_params=pltpu.CompilerParams(collective_id=1, has_side_effects=True, vmem_limit_bytes=VMEM_LIMIT),
         name="regroup",
     )(base, rows, slots, bare_pos)

time: 54 us -> 50 us (0.926)
  Pallas kernels: 52.5 us -> 48.5 us
    pallas_call x1, Pallas kernels: 21.4 us -> 17.8 us  [on_device(): pl.pallas_call(functools.partial(regroup_kernel, count), out_shape=(squar...]
where the time goes in v6:
time: 50 us; the launch traced here: 49.8 us
  Pallas kernels  48.5 us (97%)
  between operations  1.3 us (3%)
    pallas_call x1, Pallas kernels, on_device(): pl.pallas_call(functools.partial(collect_kernel, count, spaces), out_shap...  20.1 us
    pallas_call x1, Pallas kernels, on_device(): pl.pallas_call(functools.partial(regroup_kernel, count), out_shape=(squar...  17.8 us
    pallas_call x1, Pallas kernels, on_device(): pl.pallas_call(chain_kernel, out_shape=(square, square), in_specs=[smem,...  8.27 us
    pallas_call x1, Pallas kernels, on_device(): pl.pallas_call(finish_kernel, out_shape=(jax.ShapeDtypeStruct((1, 1, widt...  2.26 us

profile of v6, /device:TPU:1, one launch (start us, length us, event | category | flops | bytes accessed | tf_op | source)
XLA Modules:
  0.0 49.8 jit_solution(5666539435488546153)
XLA Ops:
  1.3 20.1 %collect.1 = (f32[4,256,256]{2,1,0:T(8,128)S(1)}, f32[4,256,256]{2,1,0:T(8,128)S(1)}, s32[32,1,1408]{2,1,0:T(1,128)S(1)}, s32[32,1,1408]{2,1,0:T(1,128)S(1)}, f3...) custom-call(f32[1,256,256]{2,1,0:T(8,128)} %diag_ref.1, f32[1,256,256]{2,1,0:T(8,128)} %coup_ref.1, s32[1,43264]{1,0:T(1,128)} %pattern_ref.1, ...), custom_call_target="tpu_custom_call" | custom-call | tf_op jit(solution)/shard_map/collect/pallas_call | solution.py:527
  21.4 8.3 %chain.1 = (f32[256,256]{1,0:T(8,128)S(1)}, f32[256,256]{1,0:T(8,128)S(1)}) custom-call(f32[1]{0:T(128)S(6)} %copy.7.shift_ref, f32[4,256,256]{2,1,0:T(8,128)S(1)} %get-tuple-element.12.diags_ref, f32[4,256,256]{2,1,0:T(8,128)S(1)} %get-tuple-element.13.coups_ref), custom_call_target="tpu_custom_call" | custom-call | tf_op jit(solution)/shard_map/chain/pallas_call | solution.py:551
  29.7 17.8 %regroup.1 = (f32[256,256]{1,0:T(8,128)S(1)}, f32[32,16,128]{2,1,0:T(8,128)S(1)}) custom-call(f32[256,256]{1,0:T(8,128)S(1)} %get-tuple-element.15.base_ref, s32[32,1,1408]{2,1,0:T(1,128)S(1)} %get-tuple-element.16.rows_ref, s32[32,1,1408]{2,1,0:T(1,128)S(1)} %get-tuple-element.17.slots_ref, f32[8,256]{1,0:T(8,128)S(1)} %get-tuple-element.18.bare_pos_ref), custom_call_target="tpu_custom_call" | custom-call | tf_op jit(solution)/shard_map/regroup/pallas_call | solution.py:561
  47.6 2.3 %finish.1 = (f32[1,1,256,256]{3,2,1,0:T(8,128)}, f32[32,1,1352]{2,1,0:T(1,128)}) custom-call(f32[256,256]{1,0:T(8,128)S(1)} %get-tuple-element.14.reduced_ref, f32[256,256]{1,0:T(8,128)S(1)} %get-tuple-element.15.base_ref, f32[256,256]{1,0:T(8,128)S(1)} %get-tuple-element.19.spread_ref, f32[32,16,128]{2,1,0:T(8,128)S(1)} %get-tuple-element.20.taken_ref, ...), custom_call_target="tpu_custom_call" | custom-call | tf_op jit(solution)/shard_map/finish/pallas_call | solution.py:574
